TPU v7x, 256 devices: a whole 4x4x8 slice. The times are simulated.
256 devices in a mesh: ctx: 64 (over z, x, core), heads: 4 (over y).
Axes of the slice: x: 4, y: 4, z: 8, core: 2. Of those that a mesh axis runs over, the one named last changes fastest.
Arguments:
- q_raw: bfloat16 [16384, 8192], P('ctx', 'heads'), may hold values from -60 to 60
- k_raw: bfloat16 [16384, 1024], P('ctx', 'heads'), may hold values from -60 to 60
- values: bfloat16 [16384, 1024], P('ctx', 'heads'), may hold values from -6 to 6
- saved_out: bfloat16 [16384, 8192], P('ctx', 'heads'), may hold values from -6 to 6
- out_grad: bfloat16 [16384, 8192], P('ctx', 'heads'), may hold values from -60 to 60
- q_gain: float32 [128], replicated, may hold values from 0.25 to 1.75
- k_gain: float32 [128], replicated, may hold values from 0.25 to 1.75
- ancestors: int32 [256, 32], P('ctx'), may hold values from -1 to 255, as said below
Outputs:
- dq_raw: bfloat16 [16384, 8192], P('ctx', 'heads')
- dk_raw: bfloat16 [16384, 1024], P('ctx', 'heads')
- dv: bfloat16 [16384, 1024], P('ctx', 'heads')
- q_gain_grad: float32 [128], replicated
- k_gain_grad: float32 [128], replicated
Inputs may be any that keep to these rules, and one draw needn't show every extreme that they name: `ancestors`: the forest is 8 trees of 32 blocks each; in tree order, tree k holds blocks (k * 32 + 256 / 64 + b) mod 256 for b = 0 to 31. Row b lists, in tree order, every block on the path from its tree's first block to b, ending with b itself, then -1s. The first 16 blocks of a tree form its prompt, each the child of the block before it; every other block's parent is a block earlier in its tree, from the prompt's last block on.
All inputs are finite; a program needn't handle non-finite values.
Results may differ from a plain program's by a relative error of at most 0.0069.
Values may be sent and summed in bfloat16 or wider, within the bound.
A program may use at most 64 MiB of HBM per device.

v0:
```python
import math

import jax
import jax.numpy as jnp
from jax import lax
from jax.sharding import PartitionSpec as P

TREE_DEV = 8


ROPE_BASE = 1000000.0
EPS = 1e-06


def passed_along(value, axis, steps):
    count = lax.axis_size(axis)
    pairs = [(source, (source + steps) % count) for source in range(count)]
    return lax.ppermute(value, axis, pairs)


def rope_tables(positions, head_dim):
    half_dim = head_dim // 2
    frequency = jnp.exp(
        jnp.arange(half_dim, dtype=jnp.float32) * (-2.0 * math.log(ROPE_BASE) / head_dim)
    )
    angles = positions.astype(jnp.float32)[:, None] * frequency[None, :]
    return (jnp.cos(angles), jnp.sin(angles))


def norm_rope(inputs, gain_vec, cos_table, sin_table):
    recip_rms = lax.rsqrt(jnp.mean(inputs * inputs, -1, keepdims=True) + EPS)
    scaled = inputs * recip_rms * gain_vec
    half_dim = inputs.shape[-1] // 2
    cos_part = cos_table[:, None, :]
    sin_part = sin_table[:, None, :]
    front_half = scaled[..., :half_dim]
    back_half = scaled[..., half_dim:]
    return jnp.concatenate(
        [
            front_half * cos_part - back_half * sin_part,
            back_half * cos_part + front_half * sin_part,
        ],
        -1,
    )


def norm_rope_back(inputs, gain_vec, cos_table, sin_table, upstream):
    half_dim = inputs.shape[-1] // 2
    cos_part = cos_table[:, None, :]
    sin_part = sin_table[:, None, :]
    front_half = upstream[..., :half_dim]
    back_half = upstream[..., half_dim:]
    unrotated = jnp.concatenate(
        [
            front_half * cos_part + back_half * sin_part,
            back_half * cos_part - front_half * sin_part,
        ],
        -1,
    )
    recip_rms = lax.rsqrt(jnp.mean(inputs * inputs, -1, keepdims=True) + EPS)
    normed = inputs * recip_rms
    gain_term = jnp.sum(unrotated * normed, axis=(0, 1))
    gain_grad = unrotated * gain_vec
    input_grad = recip_rms * (gain_grad - normed * jnp.mean(gain_grad * normed, -1, keepdims=True))
    return (input_grad, gain_term)


def on_device(q_raw, k_raw, values, saved_out, out_grad, q_gain, k_gain, ancestors):
    tokens_here = q_raw.shape[0]
    head_dim = q_gain.shape[0]
    kv_local = k_raw.shape[1] // head_dim
    group_size = q_raw.shape[1] // (kv_local * head_dim)
    block_count = ancestors.shape[0]
    block_len = tokens_here // block_count
    cycle_size = lax.axis_size("ctx")
    my_index = lax.axis_index("ctx")
    hop_count = TREE_DEV - 1
    inv_root = 1.0 / math.sqrt(head_dim)
    offsets = jnp.arange(block_len, dtype=jnp.int32)
    depth_count = jnp.sum((ancestors >= 0).astype(jnp.int32), 1)
    positions = (((depth_count - 1) * block_len)[:, None] + offsets[None, :]).reshape(tokens_here)
    cos_table, sin_table = rope_tables(positions, head_dim)
    q_float = q_raw.astype(jnp.float32).reshape(tokens_here, kv_local * group_size, head_dim)
    k_float = k_raw.astype(jnp.float32).reshape(tokens_here, kv_local, head_dim)
    q_rot = norm_rope(q_float, q_gain, cos_table, sin_table).astype(jnp.bfloat16)
    q_rot = q_rot.reshape(tokens_here, kv_local, group_size, head_dim)
    k_rot = norm_rope(k_float, k_gain, cos_table, sin_table).astype(jnp.bfloat16)
    v_heads = values.reshape(tokens_here, kv_local, head_dim)
    grad_heads = out_grad.reshape(tokens_here, kv_local, group_size, head_dim)
    out_heads = saved_out.reshape(tokens_here, kv_local, group_size, head_dim)
    row_delta = jnp.einsum(
        "ikgd,ikgd->kgi", grad_heads, out_heads, preferred_element_type=jnp.float32
    )
    key_value = jnp.stack((k_rot, v_heads), 1)
    local_tok = jnp.arange(tokens_here, dtype=jnp.int32)

    def visible(source):
        key_blocks = source * block_count + jnp.arange(block_count, dtype=jnp.int32)
        block_vis = jnp.any(ancestors[:, :, None] == key_blocks[None, None, :], axis=1)
        token_vis = jnp.repeat(jnp.repeat(block_vis, block_len, 0), block_len, 1)
        causal = (local_tok[None, :] <= local_tok[:, None]) | (source != my_index)
        return (token_vis & causal, jnp.any(block_vis))

    def scores_of(key_rot):
        return (
            jnp.einsum("ikgd,jkd->kgij", q_rot, key_rot, preferred_element_type=jnp.float32)
            * inv_root
        )

    def add_mass(exp_mass, key_rot, allowed):
        expo = jnp.where(allowed[None, None], jnp.exp(scores_of(key_rot)), 0.0)
        return exp_mass + jnp.sum(expo, -1)

    def accumulate(exp_mass, key_rot, allowed):
        return add_mass(exp_mass, key_rot, allowed)

    own_allowed, own_touched = visible(my_index)
    exp_mass = add_mass(
        jnp.zeros((kv_local, group_size, tokens_here), jnp.float32), k_rot, own_allowed
    )

    def forward_step(hop_index, loop_state):
        mass_now, moving = loop_state
        moving = passed_along(moving, "ctx", 1)
        allowed, touched = visible((my_index - hop_index) % cycle_size)
        return (accumulate(mass_now, moving, allowed), moving)

    exp_mass, _ = lax.fori_loop(1, hop_count + 1, forward_step, (exp_mass, k_rot))
    log_mass = jnp.log(exp_mass)

    def grad_terms(key_rot, val_rot, allowed):
        weights = jnp.where(
            allowed[None, None], jnp.exp(scores_of(key_rot) - log_mass[..., None]), 0.0
        )
        weights_low = weights.astype(jnp.bfloat16)
        grad_prob = jnp.einsum(
            "ikgd,jkd->kgij", grad_heads, val_rot, preferred_element_type=jnp.float32
        )
        dscore = (weights * (grad_prob - row_delta[..., None]) * inv_root).astype(jnp.bfloat16)
        dq_part = jnp.einsum("kgij,jkd->ikgd", dscore, key_rot, preferred_element_type=jnp.float32)
        dk_part = jnp.einsum("kgij,ikgd->jkd", dscore, q_rot, preferred_element_type=jnp.float32)
        dv_part = jnp.einsum(
            "kgij,ikgd->jkd", weights_low, grad_heads, preferred_element_type=jnp.float32
        )
        return (dq_part, jnp.stack((dk_part, dv_part), 1))

    def pair_terms(moving, allowed):
        return grad_terms(moving[:, 0], moving[:, 1], allowed)

    dq_acc, own_part = grad_terms(k_rot, v_heads, own_allowed)
    key_grads = own_part

    def back_step(hop_index, loop_state):
        dq_now, grads_now, moving = loop_state
        moving = passed_along(moving, "ctx", 1)
        source = (my_index - hop_index) % cycle_size
        allowed, touched = visible(source)
        dq_part, kv_part = pair_terms(moving, allowed)
        grads_now = passed_along(grads_now, "ctx", 1) + kv_part
        return (dq_now + dq_part, grads_now, moving)

    dq_acc, key_grads, _ = lax.fori_loop(
        1, hop_count + 1, back_step, (dq_acc, key_grads, key_value)
    )
    key_grads = passed_along(key_grads, "ctx", -hop_count)
    dq_rot = dq_acc.reshape(tokens_here, kv_local * group_size, head_dim)
    dq_input, q_gain_part = norm_rope_back(q_float, q_gain, cos_table, sin_table, dq_rot)
    dk_input, k_gain_part = norm_rope_back(k_float, k_gain, cos_table, sin_table, key_grads[:, 0])
    q_gain_grad, k_gain_grad = lax.psum((q_gain_part, k_gain_part), ("ctx", "heads"))
    dq_raw = dq_input.astype(jnp.bfloat16).reshape(tokens_here, kv_local * group_size * head_dim)
    dk_raw = dk_input.astype(jnp.bfloat16).reshape(tokens_here, kv_local * head_dim)
    dv = key_grads[:, 1].astype(jnp.bfloat16).reshape(tokens_here, kv_local * head_dim)
    return (dq_raw, dk_raw, dv, q_gain_grad, k_gain_grad)


def solution(mesh):
    in_specs = (
        P("ctx", "heads"),
        P("ctx", "heads"),
        P("ctx", "heads"),
        P("ctx", "heads"),
        P("ctx", "heads"),
        P(),
        P(),
        P("ctx", None),
    )
    out_specs = (P("ctx", "heads"), P("ctx", "heads"), P("ctx", "heads"), P(), P())
    return jax.shard_map(
        on_device, mesh=mesh, in_specs=in_specs, out_specs=out_specs, check_vma=False
    )
```

profile of v0, /device:TPU:1, one launch (start us, length us, event | category | flops | bytes accessed | tf_op | source)
XLA Modules:
  0.0 316.6 jit_solution(3900875006757037314)
XLA Ops:
  11.5 2.9 fusion.29
  14.4 59.1 %while.38 = (s32[]{:T(128)}, f32[2,8,256]{2,1,0:T(8,128)S(1)}, bf16[256,2,128]{2,0,1:T(8,128)(2,1)S(1)}, s32[4,32]{1,0:T(4,128)S(1)}, s32[]{:T(128)}, /*index=5*...) while((s32[]{:T(128)}, f32[2,8,256]{2,1,0:T(8,128)S(1)}, ...), condition=%wide.region_8.9_spmd.clone, body=%wide.region_5.8_spmd.clone.sunk | while | flops 271778816 | bytes 2167688 | solution.py:128
  14.4 2.6 collective-permute-start
  20.0 2.5 collective-permute-start
  23.1 4.9 %collective-permute-done = bf16[256,2,128]{2,0,1:T(8,128)(2,1)S(1)} collective-permute-done((bf16[256,2,128]{2,0,1:T(8,128)(2,1)S(1)}, bf16[256,2,128]{2,0,1:T(8,128)(2,1)S(1)}, u32[]{:S(2)}, u32[]{:S(2)}) %collective-permute-start) | collective-permute-done | bytes 131104 | tf_op jit(solution)/shard_map/while/body/eval_jaxpr/ppermute | solution.py:18
  29.8 7.1 %collective-permute-done = bf16[256,2,128]{2,0,1:T(8,128)(2,1)S(1)} collective-permute-done((bf16[256,2,128]{2,0,1:T(8,128)(2,1)S(1)}, bf16[256,2,128]{2,0,1:T(8,128)(2,1)S(1)}, u32[]{:S(2)}, u32[]{:S(2)}) %collective-permute-start) | collective-permute-done | bytes 131104 | tf_op jit(solution)/shard_map/while/body/eval_jaxpr/ppermute | solution.py:18
  38.7 7.1 %collective-permute-done = bf16[256,2,128]{2,0,1:T(8,128)(2,1)S(1)} collective-permute-done((bf16[256,2,128]{2,0,1:T(8,128)(2,1)S(1)}, bf16[256,2,128]{2,0,1:T(8,128)(2,1)S(1)}, u32[]{:S(2)}, u32[]{:S(2)}) %collective-permute-start) | collective-permute-done | bytes 131104 | tf_op jit(solution)/shard_map/while/body/eval_jaxpr/ppermute | solution.py:18
  47.5 7.1 %collective-permute-done = bf16[256,2,128]{2,0,1:T(8,128)(2,1)S(1)} collective-permute-done((bf16[256,2,128]{2,0,1:T(8,128)(2,1)S(1)}, bf16[256,2,128]{2,0,1:T(8,128)(2,1)S(1)}, u32[]{:S(2)}, u32[]{:S(2)}) %collective-permute-start) | collective-permute-done | bytes 131104 | tf_op jit(solution)/shard_map/while/body/eval_jaxpr/ppermute | solution.py:18
  56.4 7.1 %collective-permute-done = bf16[256,2,128]{2,0,1:T(8,128)(2,1)S(1)} collective-permute-done((bf16[256,2,128]{2,0,1:T(8,128)(2,1)S(1)}, bf16[256,2,128]{2,0,1:T(8,128)(2,1)S(1)}, u32[]{:S(2)}, u32[]{:S(2)}) %collective-permute-start) | collective-permute-done | bytes 131104 | tf_op jit(solution)/shard_map/while/body/eval_jaxpr/ppermute | solution.py:18
  65.3 7.1 %collective-permute-done = bf16[256,2,128]{2,0,1:T(8,128)(2,1)S(1)} collective-permute-done((bf16[256,2,128]{2,0,1:T(8,128)(2,1)S(1)}, bf16[256,2,128]{2,0,1:T(8,128)(2,1)S(1)}, u32[]{:S(2)}, u32[]{:S(2)}) %collective-permute-start) | collective-permute-done | bytes 131104 | tf_op jit(solution)/shard_map/while/body/eval_jaxpr/ppermute | solution.py:18
  79.2 3.3 %fusion.40 = f32[256,1,2,128]{0,3,2,1:T(8,128)S(1)} fusion(bf16[256,2,8,128]{0,3,2,1:T(8,128)(2,1)S(1)} %bitcast.262, f32[2,256,256,8]{2,1,3,0:T(8,128)} %get-tuple-element.597, f32[2,8,256]{2,1,0:T(8,128)S(1)} %copy-done.24, pred[256,256]{0,1:T(8,128)(4,1)S(1)} %copy-done.21), kind=kOutput, calls=%fused_computation.66 | convolution fusion | flops 272629760 | bytes 5586944 | tf_op jit(solution)/shard_map/kgij,ikgd->jkd/dot_general | solution.py:142
  89.9 1.9 copy.98
  95.2 123.4 %while.39 = (s32[]{:T(128)}, f32[256,2,8,128]{3,0,2,1:T(8,128)S(1)}, f32[256,2,2,128]{3,0,2,1:T(8,128)}, bf16[256,2,2,128]{3,0,2,1:T(8,128)(2,1)}, s32[4,32]{1,0...) while((s32[]{:T(128)}, ...), condition=%wide.region_11.12_spmd.clone, body=%wide.region_9.11_spmd.clone.sunk | while | flops 1354695680 | bytes 37999652 | solution.py:162
  96.9 6.4 %collective-permute-done.1 = bf16[256,2,2,128]{3,0,2,1:T(8,128)(2,1)S(1)} collective-permute-done((bf16[256,2,2,128]{3,0,2,1:T(8,128)(2,1)}, bf16[256,2,2,128]{3,0,2,1:T(8,128)(2,1)S(1)}, u32[]{:S(2)}, u32[]{:S(2)}) %collective-permute-start.1) | collective-permute-done | bytes 262176 | tf_op jit(solution)/shard_map/while/body/eval_jaxpr/ppermute | solution.py:18
  113.5 7.6 %collective-permute-done.1 = bf16[256,2,2,128]{3,0,2,1:T(8,128)(2,1)S(1)} collective-permute-done((bf16[256,2,2,128]{3,0,2,1:T(8,128)(2,1)}, bf16[256,2,2,128]{3,0,2,1:T(8,128)(2,1)S(1)}, u32[]{:S(2)}, u32[]{:S(2)}) %collective-permute-start.1) | collective-permute-done | bytes 262176 | tf_op jit(solution)/shard_map/while/body/eval_jaxpr/ppermute | solution.py:18
  131.3 7.6 %collective-permute-done.1 = bf16[256,2,2,128]{3,0,2,1:T(8,128)(2,1)S(1)} collective-permute-done((bf16[256,2,2,128]{3,0,2,1:T(8,128)(2,1)}, bf16[256,2,2,128]{3,0,2,1:T(8,128)(2,1)S(1)}, u32[]{:S(2)}, u32[]{:S(2)}) %collective-permute-start.1) | collective-permute-done | bytes 262176 | tf_op jit(solution)/shard_map/while/body/eval_jaxpr/ppermute | solution.py:18
  149.1 7.6 %collective-permute-done.1 = bf16[256,2,2,128]{3,0,2,1:T(8,128)(2,1)S(1)} collective-permute-done((bf16[256,2,2,128]{3,0,2,1:T(8,128)(2,1)}, bf16[256,2,2,128]{3,0,2,1:T(8,128)(2,1)S(1)}, u32[]{:S(2)}, u32[]{:S(2)}) %collective-permute-start.1) | collective-permute-done | bytes 262176 | tf_op jit(solution)/shard_map/while/body/eval_jaxpr/ppermute | solution.py:18
  166.9 7.6 %collective-permute-done.1 = bf16[256,2,2,128]{3,0,2,1:T(8,128)(2,1)S(1)} collective-permute-done((bf16[256,2,2,128]{3,0,2,1:T(8,128)(2,1)}, bf16[256,2,2,128]{3,0,2,1:T(8,128)(2,1)S(1)}, u32[]{:S(2)}, u32[]{:S(2)}) %collective-permute-start.1) | collective-permute-done | bytes 262176 | tf_op jit(solution)/shard_map/while/body/eval_jaxpr/ppermute | solution.py:18
  184.7 7.6 %collective-permute-done.1 = bf16[256,2,2,128]{3,0,2,1:T(8,128)(2,1)S(1)} collective-permute-done((bf16[256,2,2,128]{3,0,2,1:T(8,128)(2,1)}, bf16[256,2,2,128]{3,0,2,1:T(8,128)(2,1)S(1)}, u32[]{:S(2)}, u32[]{:S(2)}) %collective-permute-start.1) | collective-permute-done | bytes 262176 | tf_op jit(solution)/shard_map/while/body/eval_jaxpr/ppermute | solution.py:18
  202.5 7.6 %collective-permute-done.1 = bf16[256,2,2,128]{3,0,2,1:T(8,128)(2,1)S(1)} collective-permute-done((bf16[256,2,2,128]{3,0,2,1:T(8,128)(2,1)}, bf16[256,2,2,128]{3,0,2,1:T(8,128)(2,1)S(1)}, u32[]{:S(2)}, u32[]{:S(2)}) %collective-permute-start.1) | collective-permute-done | bytes 262176 | tf_op jit(solution)/shard_map/while/body/eval_jaxpr/ppermute | solution.py:18
  220.2 2.5 multiply_add_fusion
  222.7 2.1 multiply_reduce_fusion.1
  226.0 3.8 %fusion.36 = (f32[2048]{0:T(1024)S(1)}, bf16[256,2048]{1,0:T(8,128)(2,1)}) fusion(bf16[256,2048]{1,0:T(8,128)(2,1)S(1)} %copy-done.3, f32[32,8,16,128]{3,2,1,0:T(8,128)S(1)} %bitcast.265, f32[32,8,16,128]{3,2,1,0:T(8,128)S(1)} %bitcast.267, f32[32,8,16,128]{3,2,1,0:T(8,128)S(1)} %bitcast.266, f32[2048]{0:T(1024)S(1)} %broadcast_bitcast_fusion), kind=kLoop, calls=%fused_computation.53 | loop fusion | flops 4716544 | bytes 8404992 | tf_op jit(solution)/shard_map/reduce_sum | solution.py:62
  232.6 84.0 %all-reduce = (f32[128]{0:T(128)}, f32[128]{0:T(128)}) all-reduce(f32[128]{0:T(128)S(1)} %bitcast_reduce_fusion, f32[128]{0:T(128)S(1)} %bitcast_reduce_fusion.1), channel_id=1, replica_groups=mesh['ctx'=64,'heads'=4] {'ctx','heads'}, use_global_device_ids=true, to_apply=%region_16.17 | all-reduce | flops 256 | bytes 2048 | tf_op jit(solution)/shard_map/psum | solution.py:169
  (344 shorter events, 116.3 us)
Async XLA Ops:
  1.8 5.1 %copy-start.6 = (f32[256,2,128]{2,0,1:T(8,128)}, f32[256,2,128]{2,0,1:T(8,128)S(1)}, u32[]{:S(2)}) copy-start(f32[256,2,128]{2,0,1:T(8,128)S(1)} %copy.83) | copy-start | bytes 786436
  14.4 59.7 %copy-start.14 = (bf16[256,2048]{1,0:T(8,128)(2,1)S(1)}, bf16[256,2048]{1,0:T(8,128)(2,1)}, u32[]{:S(2)}) copy-start(bf16[256,2048]{1,0:T(8,128)(2,1)} %param.16) | copy-start | bytes 3145732
  14.4 4.5 %collective-permute-start = (bf16[256,2,128]{2,0,1:T(8,128)(2,1)S(1)}, bf16[256,2,128]{2,0,1:T(8,128)(2,1)S(1)}, u32[]{:S(2)}, u32[]{:S(2)}) collective-permute-start(bf16[256,2,128]{2,0,1:T(8,128)(2,1)S(1)} %get-tuple-element.709), channel_id=1, source_target_pairs={{0,4},{4,8},{8,12},{12,16},{16,20},{20,24},{24,28},{28,32},{32,36}... | collective-permute-start | bytes 393224 | tf_op jit(solution)/shard_map/while/body/eval_jaxpr/ppermute | solution.py:18
  20.0 8.0 %collective-permute-start = (bf16[256,2,128]{2,0,1:T(8,128)(2,1)S(1)}, bf16[256,2,128]{2,0,1:T(8,128)(2,1)S(1)}, u32[]{:S(2)}, u32[]{:S(2)}) collective-permute-start(bf16[256,2,128]{2,0,1:T(8,128)(2,1)S(1)} %get-tuple-element.709), channel_id=1, source_target_pairs={{0,4},{4,8},{8,12},{12,16},{16,20},{20,24},{24,28},{28,32},{32,36}... | collective-permute-start | bytes 393224 | tf_op jit(solution)/shard_map/while/body/eval_jaxpr/ppermute | solution.py:18
  29.1 7.8 %collective-permute-start = (bf16[256,2,128]{2,0,1:T(8,128)(2,1)S(1)}, bf16[256,2,128]{2,0,1:T(8,128)(2,1)S(1)}, u32[]{:S(2)}, u32[]{:S(2)}) collective-permute-start(bf16[256,2,128]{2,0,1:T(8,128)(2,1)S(1)} %get-tuple-element.709), channel_id=1, source_target_pairs={{0,4},{4,8},{8,12},{12,16},{16,20},{20,24},{24,28},{28,32},{32,36}... | collective-permute-start | bytes 393224 | tf_op jit(solution)/shard_map/while/body/eval_jaxpr/ppermute | solution.py:18
  38.0 7.8 %collective-permute-start = (bf16[256,2,128]{2,0,1:T(8,128)(2,1)S(1)}, bf16[256,2,128]{2,0,1:T(8,128)(2,1)S(1)}, u32[]{:S(2)}, u32[]{:S(2)}) collective-permute-start(bf16[256,2,128]{2,0,1:T(8,128)(2,1)S(1)} %get-tuple-element.709), channel_id=1, source_target_pairs={{0,4},{4,8},{8,12},{12,16},{16,20},{20,24},{24,28},{28,32},{32,36}... | collective-permute-start | bytes 393224 | tf_op jit(solution)/shard_map/while/body/eval_jaxpr/ppermute | solution.py:18
  46.9 7.8 %collective-permute-start = (bf16[256,2,128]{2,0,1:T(8,128)(2,1)S(1)}, bf16[256,2,128]{2,0,1:T(8,128)(2,1)S(1)}, u32[]{:S(2)}, u32[]{:S(2)}) collective-permute-start(bf16[256,2,128]{2,0,1:T(8,128)(2,1)S(1)} %get-tuple-element.709), channel_id=1, source_target_pairs={{0,4},{4,8},{8,12},{12,16},{16,20},{20,24},{24,28},{28,32},{32,36}... | collective-permute-start | bytes 393224 | tf_op jit(solution)/shard_map/while/body/eval_jaxpr/ppermute | solution.py:18
  55.7 7.8 %collective-permute-start = (bf16[256,2,128]{2,0,1:T(8,128)(2,1)S(1)}, bf16[256,2,128]{2,0,1:T(8,128)(2,1)S(1)}, u32[]{:S(2)}, u32[]{:S(2)}) collective-permute-start(bf16[256,2,128]{2,0,1:T(8,128)(2,1)S(1)} %get-tuple-element.709), channel_id=1, source_target_pairs={{0,4},{4,8},{8,12},{12,16},{16,20},{20,24},{24,28},{28,32},{32,36}... | collective-permute-start | bytes 393224 | tf_op jit(solution)/shard_map/while/body/eval_jaxpr/ppermute | solution.py:18
  64.6 7.8 %collective-permute-start = (bf16[256,2,128]{2,0,1:T(8,128)(2,1)S(1)}, bf16[256,2,128]{2,0,1:T(8,128)(2,1)S(1)}, u32[]{:S(2)}, u32[]{:S(2)}) collective-permute-start(bf16[256,2,128]{2,0,1:T(8,128)(2,1)S(1)} %get-tuple-element.709), channel_id=1, source_target_pairs={{0,4},{4,8},{8,12},{12,16},{16,20},{20,24},{24,28},{28,32},{32,36}... | collective-permute-start | bytes 393224 | tf_op jit(solution)/shard_map/while/body/eval_jaxpr/ppermute | solution.py:18
  95.2 8.1 %collective-permute-start.1 = (bf16[256,2,2,128]{3,0,2,1:T(8,128)(2,1)}, bf16[256,2,2,128]{3,0,2,1:T(8,128)(2,1)S(1)}, u32[]{:S(2)}, u32[]{:S(2)}) collective-permute-start(bf16[256,2,2,128]{3,0,2,1:T(8,128)(2,1)} %get-tuple-element.747), channel_id=1, source_target_pairs={{0,4},{4,8},{8,12},{12,16},{16,20},{20,24},{24,28},{28,32},{32,36}... | collective-permute-start | bytes 786440 | tf_op jit(solution)/shard_map/while/body/eval_jaxpr/ppermute | solution.py:18
  95.2 14.7 %collective-permute-start.2 = (f32[256,2,2,128]{3,0,2,1:T(8,128)}, f32[256,2,2,128]{3,0,2,1:T(8,128)}, u32[]{:S(2)}, u32[]{:S(2)}) collective-permute-start(f32[256,2,2,128]{3,0,2,1:T(8,128)} %get-tuple-element.746), channel_id=1, source_target_pairs={{0,4},{4,8},{8,12},{12,16},{16,20},{20,24},{24,28},{28,32},{32,36}... | collective-permute-start | bytes 1572872 | tf_op jit(solution)/shard_map/while/body/eval_jaxpr/ppermute | solution.py:18
  111.8 9.3 %collective-permute-start.1 = (bf16[256,2,2,128]{3,0,2,1:T(8,128)(2,1)}, bf16[256,2,2,128]{3,0,2,1:T(8,128)(2,1)S(1)}, u32[]{:S(2)}, u32[]{:S(2)}) collective-permute-start(bf16[256,2,2,128]{3,0,2,1:T(8,128)(2,1)} %get-tuple-element.747), channel_id=1, source_target_pairs={{0,4},{4,8},{8,12},{12,16},{16,20},{20,24},{24,28},{28,32},{32,36}... | collective-permute-start | bytes 786440 | tf_op jit(solution)/shard_map/while/body/eval_jaxpr/ppermute | solution.py:18
  111.8 15.9 %collective-permute-start.2 = (f32[256,2,2,128]{3,0,2,1:T(8,128)}, f32[256,2,2,128]{3,0,2,1:T(8,128)}, u32[]{:S(2)}, u32[]{:S(2)}) collective-permute-start(f32[256,2,2,128]{3,0,2,1:T(8,128)} %get-tuple-element.746), channel_id=1, source_target_pairs={{0,4},{4,8},{8,12},{12,16},{16,20},{20,24},{24,28},{28,32},{32,36}... | collective-permute-start | bytes 1572872 | tf_op jit(solution)/shard_map/while/body/eval_jaxpr/ppermute | solution.py:18
  129.6 9.3 %collective-permute-start.1 = (bf16[256,2,2,128]{3,0,2,1:T(8,128)(2,1)}, bf16[256,2,2,128]{3,0,2,1:T(8,128)(2,1)S(1)}, u32[]{:S(2)}, u32[]{:S(2)}) collective-permute-start(bf16[256,2,2,128]{3,0,2,1:T(8,128)(2,1)} %get-tuple-element.747), channel_id=1, source_target_pairs={{0,4},{4,8},{8,12},{12,16},{16,20},{20,24},{24,28},{28,32},{32,36}... | collective-permute-start | bytes 786440 | tf_op jit(solution)/shard_map/while/body/eval_jaxpr/ppermute | solution.py:18
  129.6 15.9 %collective-permute-start.2 = (f32[256,2,2,128]{3,0,2,1:T(8,128)}, f32[256,2,2,128]{3,0,2,1:T(8,128)}, u32[]{:S(2)}, u32[]{:S(2)}) collective-permute-start(f32[256,2,2,128]{3,0,2,1:T(8,128)} %get-tuple-element.746), channel_id=1, source_target_pairs={{0,4},{4,8},{8,12},{12,16},{16,20},{20,24},{24,28},{28,32},{32,36}... | collective-permute-start | bytes 1572872 | tf_op jit(solution)/shard_map/while/body/eval_jaxpr/ppermute | solution.py:18
  147.4 9.3 %collective-permute-start.1 = (bf16[256,2,2,128]{3,0,2,1:T(8,128)(2,1)}, bf16[256,2,2,128]{3,0,2,1:T(8,128)(2,1)S(1)}, u32[]{:S(2)}, u32[]{:S(2)}) collective-permute-start(bf16[256,2,2,128]{3,0,2,1:T(8,128)(2,1)} %get-tuple-element.747), channel_id=1, source_target_pairs={{0,4},{4,8},{8,12},{12,16},{16,20},{20,24},{24,28},{28,32},{32,36}... | collective-permute-start | bytes 786440 | tf_op jit(solution)/shard_map/while/body/eval_jaxpr/ppermute | solution.py:18
  147.4 15.9 %collective-permute-start.2 = (f32[256,2,2,128]{3,0,2,1:T(8,128)}, f32[256,2,2,128]{3,0,2,1:T(8,128)}, u32[]{:S(2)}, u32[]{:S(2)}) collective-permute-start(f32[256,2,2,128]{3,0,2,1:T(8,128)} %get-tuple-element.746), channel_id=1, source_target_pairs={{0,4},{4,8},{8,12},{12,16},{16,20},{20,24},{24,28},{28,32},{32,36}... | collective-permute-start | bytes 1572872 | tf_op jit(solution)/shard_map/while/body/eval_jaxpr/ppermute | solution.py:18
  165.2 9.3 %collective-permute-start.1 = (bf16[256,2,2,128]{3,0,2,1:T(8,128)(2,1)}, bf16[256,2,2,128]{3,0,2,1:T(8,128)(2,1)S(1)}, u32[]{:S(2)}, u32[]{:S(2)}) collective-permute-start(bf16[256,2,2,128]{3,0,2,1:T(8,128)(2,1)} %get-tuple-element.747), channel_id=1, source_target_pairs={{0,4},{4,8},{8,12},{12,16},{16,20},{20,24},{24,28},{28,32},{32,36}... | collective-permute-start | bytes 786440 | tf_op jit(solution)/shard_map/while/body/eval_jaxpr/ppermute | solution.py:18
  165.2 15.9 %collective-permute-start.2 = (f32[256,2,2,128]{3,0,2,1:T(8,128)}, f32[256,2,2,128]{3,0,2,1:T(8,128)}, u32[]{:S(2)}, u32[]{:S(2)}) collective-permute-start(f32[256,2,2,128]{3,0,2,1:T(8,128)} %get-tuple-element.746), channel_id=1, source_target_pairs={{0,4},{4,8},{8,12},{12,16},{16,20},{20,24},{24,28},{28,32},{32,36}... | collective-permute-start | bytes 1572872 | tf_op jit(solution)/shard_map/while/body/eval_jaxpr/ppermute | solution.py:18
  183.0 9.3 %collective-permute-start.1 = (bf16[256,2,2,128]{3,0,2,1:T(8,128)(2,1)}, bf16[256,2,2,128]{3,0,2,1:T(8,128)(2,1)S(1)}, u32[]{:S(2)}, u32[]{:S(2)}) collective-permute-start(bf16[256,2,2,128]{3,0,2,1:T(8,128)(2,1)} %get-tuple-element.747), channel_id=1, source_target_pairs={{0,4},{4,8},{8,12},{12,16},{16,20},{20,24},{24,28},{28,32},{32,36}... | collective-permute-start | bytes 786440 | tf_op jit(solution)/shard_map/while/body/eval_jaxpr/ppermute | solution.py:18
  183.0 15.9 %collective-permute-start.2 = (f32[256,2,2,128]{3,0,2,1:T(8,128)}, f32[256,2,2,128]{3,0,2,1:T(8,128)}, u32[]{:S(2)}, u32[]{:S(2)}) collective-permute-start(f32[256,2,2,128]{3,0,2,1:T(8,128)} %get-tuple-element.746), channel_id=1, source_target_pairs={{0,4},{4,8},{8,12},{12,16},{16,20},{20,24},{24,28},{28,32},{32,36}... | collective-permute-start | bytes 1572872 | tf_op jit(solution)/shard_map/while/body/eval_jaxpr/ppermute | solution.py:18
  200.8 9.3 %collective-permute-start.1 = (bf16[256,2,2,128]{3,0,2,1:T(8,128)(2,1)}, bf16[256,2,2,128]{3,0,2,1:T(8,128)(2,1)S(1)}, u32[]{:S(2)}, u32[]{:S(2)}) collective-permute-start(bf16[256,2,2,128]{3,0,2,1:T(8,128)(2,1)} %get-tuple-element.747), channel_id=1, source_target_pairs={{0,4},{4,8},{8,12},{12,16},{16,20},{20,24},{24,28},{28,32},{32,36}... | collective-permute-start | bytes 786440 | tf_op jit(solution)/shard_map/while/body/eval_jaxpr/ppermute | solution.py:18
  200.8 15.9 %collective-permute-start.2 = (f32[256,2,2,128]{3,0,2,1:T(8,128)}, f32[256,2,2,128]{3,0,2,1:T(8,128)}, u32[]{:S(2)}, u32[]{:S(2)}) collective-permute-start(f32[256,2,2,128]{3,0,2,1:T(8,128)} %get-tuple-element.746), channel_id=1, source_target_pairs={{0,4},{4,8},{8,12},{12,16},{16,20},{20,24},{24,28},{28,32},{32,36}... | collective-permute-start | bytes 1572872 | tf_op jit(solution)/shard_map/while/body/eval_jaxpr/ppermute | solution.py:18
  218.6 11.3 %collective-permute-start.3 = (f32[256,2,2,128]{3,0,2,1:T(8,128)}, f32[256,2,2,128]{3,0,2,1:T(8,128)S(1)}, u32[]{:S(2)}, u32[]{:S(2)}) collective-permute-start(f32[256,2,2,128]{3,0,2,1:T(8,128)} %get-tuple-element.450), channel_id=1, source_target_pairs={{0,228},{4,232},{8,236},{12,240},{16,244},{20,248},{24,252},{28,0}... | collective-permute-start | bytes 1572872 | tf_op jit(solution)/shard_map/ppermute | solution.py:18
  (47 other events, 81.6 us)
where the time goes:
time: 318 us; the launch traced here: 317 us
  waiting for transfers between devices  94.1 us (30%)
  blocking collectives  84 us (26%)
  matrix products  54.6 us (17%)
  other arithmetic  39.4 us (12%)
  local copies, waits for them, and re-layouts  36.9 us (12%)
  starting transfers between devices  5.57 us (2%)
    ppermute x22, waiting for transfers between devices, passed_along(): return lax.ppermute(value, axis, pairs)  94.1 us
    psum x1, blocking collectives, on_device(): lax.psum((q_gain_part, k_gain_part), ('ctx', 'heads'))  84 us
    dot_general x15, matrix products, scores_of(): jnp.einsum('ikgd,jkd->kgij', q_rot, key_rot, preferred_element_type=jnp.f...  15 us
    unnamed x68, local copies, waits for them, and re-layouts  13.6 us
    add x7, other arithmetic, back_step(): grads_now = passed_along(grads_now, 'ctx', 1) + kv_part  13.4 us
    dot_general x8, matrix products, grad_terms(): jnp.einsum('ikgd,jkd->kgij', grad_heads, val_rot, preferred_element_type=...  12.1 us
    dot_general x8, matrix products, grad_terms(): jnp.einsum('kgij,jkd->ikgd', dscore, key_rot, preferred_element_type=jnp....  11.6 us
    dot_general x8, matrix products, grad_terms(): jnp.einsum('kgij,ikgd->jkd', weights_low, grad_heads, preferred_element_t...  10 us
  transfers between devices with their start and end apart: 22, of which 14 were waited for; matrix products, arithmetic and copies ran while one was open for 22% of the time, Pallas kernels for 0%

commit v1 on v0

v1 whole, which is shorter than its diff:
```python
import functools
import math

import jax
import jax.numpy as jnp
import numpy as np
from jax import lax
from jax.experimental import pallas as pl
from jax.experimental.pallas import tpu as pltpu
from jax.sharding import PartitionSpec as P

ROPE_BASE = 1000000.0
EPS = 1e-06
T = 256
D = 128
G = 8
BLK = 64
HALF = G * D
INV_ROOT = 1.0 / math.sqrt(D)
EXP_SCALE = INV_ROOT * math.log2(math.e)
F32 = jnp.float32
BF16 = jnp.bfloat16


def nn(a, b):
    return lax.dot_general(a, b, (((1,), (0,)), ((), ())), preferred_element_type=F32)


def nt(a, b):
    return lax.dot_general(a, b, (((1,), (1,)), ((), ())), preferred_element_type=F32)


def kernel(
    nz, q_hbm, k_ref, v_ref, so_hbm, do_hbm, qg_ref, kg_ref, anc_ref, fr_ref,
    dq_hbm, dk_ref, dv_ref, qgg_ref, kgg_ref,
    qx, dox, sox, kv, kvs, kt, aux, cosn, sinn, knorm, krec,
    qrt, qnt, qr, dot, dlt, dqt, esum, eb, gb, mask, eye, dkv, pbuf, red, dqo,
    qga, acc, ar1, ar2, ar3,
    lsem, xs, xr, kvs_sem, kvr_sem, ps_sem, pr_sem, os_sem, or_sem,
    s1, r1, s2, r2, s3, r3,
):
    c = lax.axis_index("ctx")
    y = lax.axis_index("heads")
    z = c // 8
    x = (c % 8) // 2
    h = c % 2
    nctx = nz * 8
    znext = (z + 1) % nz
    zprev = (z + nz - 1) % nz
    partner = c + 1 - 2 * h
    first = x == 0

    def rcopy(src, dst, ssem, rsem, ctx, heads=None):
        return pltpu.make_async_remote_copy(
            src_ref=src, dst_ref=dst, send_sem=ssem, recv_sem=rsem,
            device_id=(ctx, y if heads is None else heads),
            device_id_type=pl.DeviceIdType.MESH,
        )

    mine = pl.ds(pl.multiple_of(h * HALF, HALF), HALF)
    other = pl.ds(pl.multiple_of((1 - h) * HALF, HALF), HALF)
    loads = [
        pltpu.make_async_copy(src.at[:, mine], dst.at[h], lsem.at[n])
        for n, (src, dst) in enumerate(((q_hbm, qx), (do_hbm, dox), (so_hbm, sox)))
    ]
    for cp in loads:
        cp.start()

    bar = pltpu.get_barrier_semaphore()

    def greet(ctx, heads=None):
        pl.semaphore_signal(
            bar, inc=1, device_id=(ctx, y if heads is None else heads),
            device_id_type=pl.DeviceIdType.MESH,
        )

    for n in range(1, 8):
        greet(z * 8 + (c % 8 + n) % 8)
    for n in range(1, 4):
        greet(c, (y + n) % 4)
    for n in range(1, nz):
        greet((c + 8 * n) % nctx)
    for n in range(2):
        greet(znext * 8 + n)

    @pl.when(first)
    def _():
        for n in range(8):
            greet(zprev * 8 + n)

    anc = anc_ref[...]
    depth = jnp.sum((anc >= 0).astype(jnp.int32), axis=1, keepdims=True)
    off = lax.broadcasted_iota(jnp.int32, (BLK, D), 0)
    pos = jnp.concatenate(
        [(depth[b : b + 1] - 1) * BLK + off for b in range(4)], axis=0
    ).astype(F32)
    ang = pos * fr_ref[...]
    lane = lax.broadcasted_iota(jnp.int32, (T, D), 1)
    cos = jnp.cos(ang)
    sin = jnp.sin(ang)
    cosn[...] = cos
    sgn = jnp.where(lane < 64, -sin, sin)
    sinn[...] = sgn
    aux[h, 0:64, :] = cos.T[0:64]
    aux[h, 64:128, :] = sin.T[0:64]
    own_tree = jnp.where(first & (h == 0), zprev, z)
    ids = (lax.broadcasted_iota(jnp.int32, (32, 32), 0) + own_tree * 32 + 4) % (nz * 32)
    aux[h, 128:160, :] = jnp.concatenate(
        [
            jnp.broadcast_to(
                jnp.max(
                    jnp.where(jnp.broadcast_to(anc[b : b + 1], (32, 32)) == ids, 1.0, 0.0),
                    axis=1, keepdims=True,
                ),
                (32, BLK),
            )
            for b in range(4)
        ],
        axis=1,
    )
    eye[...] = jnp.where(
        lax.broadcasted_iota(jnp.int32, (T, T), 0) == lax.broadcasted_iota(jnp.int32, (T, T), 1),
        1.0, 0.0,
    ).astype(BF16)
    own_slot = jnp.where(first, 7 + h, 2 * x - 1 + h)
    other_slot = jnp.where(first, 8 - h, 2 * x - h)
    for hh in range(2):
        kf = k_ref[:, hh * D : (hh + 1) * D].astype(F32)
        rec = lax.rsqrt(jnp.mean(kf * kf, -1, keepdims=True) + EPS)
        normed = kf * rec
        scaled = normed * kg_ref[...]
        knorm[hh] = normed
        krec[hh] = jnp.broadcast_to(rec, (T, D))
        kvs[hh, 0] = (scaled * cos + pltpu.roll(scaled, 64, 1) * sgn).astype(BF16)
        kvs[hh, 1] = v_ref[:, hh * D : (hh + 1) * D]
    kv[own_slot] = kvs[h]
    dqt[...] = jnp.zeros_like(dqt)
    esum[...] = jnp.zeros_like(esum)
    qga[...] = jnp.zeros_like(qga)

    pl.semaphore_wait(bar, jnp.where(first, 8, 0) + (7 + 3 + nz - 1 + 2))

    kv_on_chip = rcopy(
        kvs.at[1 - h], kv.at[own_slot], kvs_sem.at[8], kvr_sem.at[own_slot], partner
    )
    xc = [
        rcopy(src.at[:, other], dst.at[h], xs.at[n], xr.at[n], partner)
        for n, (src, dst) in enumerate(((q_hbm, qx), (do_hbm, dox), (so_hbm, sox)))
    ]
    auxc = rcopy(aux.at[h], aux.at[h], xs.at[3], xr.at[3], partner)
    kv_on_chip.start()
    auxc.start()
    for cp in xc:
        cp.start()

    source = ~(first & (h == 0))
    position = jnp.where(first, 0, 2 * x - 1 + h)

    def kv_sends(act):
        for j in range(4):
            dest = znext * 8 if j == 0 else z * 8 + 2 * j
            ok = source & (True if j == 0 else j > x)

            @pl.when(ok)
            def _():
                for hh in range(2):
                    act(
                        rcopy(
                            kvs.at[hh], kv.at[position], kvs_sem.at[2 * j + hh],
                            kvr_sem.at[position], dest + hh,
                        )
                    )

    kv_sends(lambda cp: cp.start())

    gain = qg_ref[...]

    def prep(dev):
        tab_c = aux[dev, 0:64, :]
        tab_s = aux[dev, 64:128, :]
        ones = jnp.ones((8, D), BF16)

        def head(g, _):
            cols = pl.ds(pl.multiple_of(g * D, D), D)
            rows = pl.ds(pl.multiple_of(g * T, T), T)
            qt = nt(eye[0:D, 0:D], qx[dev, :, cols])
            rec = lax.rsqrt(jnp.mean(qt * qt, 0, keepdims=True) + EPS)
            normed = qt * rec
            qnt[dev, g] = normed
            qr[dev, g] = rec
            scaled = normed * gain
            a, b = scaled[0:64], scaled[64:128]
            qrt[dev, :, rows] = jnp.concatenate(
                [a * tab_c - b * tab_s, b * tab_c + a * tab_s], 0
            ).astype(BF16)
            grad = dox[dev, :, cols]
            dot[dev, :, rows] = nt(eye[0:D, 0:D], grad).astype(BF16)
            prod = grad.astype(F32) * sox[dev, :, cols].astype(F32)
            hi = prod.astype(BF16)
            lo = (prod - hi.astype(F32)).astype(BF16)
            dlt[dev, g] = (nt(ones, hi) + nt(ones, lo))[0:1]
            return 0

        lax.fori_loop(0, G, head, 0)

    def unit(order):
        early = order <= 1
        swapped = jnp.where(early, jnp.where(order == 0, 1 - h, h), order)
        slot = jnp.where(first, 8 - swapped, 2 * x - (swapped + 1) // 2)
        dev = jnp.where(first, jnp.where(swapped == 0, 1, 0), 1 - swapped % 2)
        return dev, slot, swapped

    def arrive(slot):
        rcopy(kvs.at[0], kv.at[slot], kvs_sem.at[0], kvr_sem.at[slot], c).wait_recv()

    def tiles(dev, slot, store, masked):
        def head(g, _):
            rows = pl.ds(pl.multiple_of(g * T, T), T)
            st = nn(kv[slot, 0], qrt[dev, :, rows])
            e = jnp.exp2(st * EXP_SCALE)
            if masked:
                e = e * mask[...]
            esum[dev, g] += jnp.sum(e, 0, keepdims=True)
            dp = nn(kv[slot, 1], dot[dev, :, rows])
            gg = (e * (dp - dlt[dev, g])).astype(BF16)
            eb[store, :, rows] = e.astype(BF16)
            gb[store, :, rows] = gg
            dqt[dev, g] += nn(kt[slot], gg)
            return 0

        lax.fori_loop(0, G, head, 0)

    def transpose_keys(slot):
        kt[slot] = nt(eye[0:D, 0:D], kv[slot, 0]).astype(BF16)

    def fill_mask(dev, index, causal):
        key = lax.broadcasted_iota(jnp.int32, (BLK, T), 0)
        tok = lax.broadcasted_iota(jnp.int32, (BLK, T), 1)
        for j in range(4):
            row = jnp.broadcast_to(aux[dev, pl.ds(128 + 4 * index + j, 1), :], (BLK, T))
            if causal:
                row = jnp.where(key + j * BLK <= tok, row, 0.0)
            mask[j * BLK : (j + 1) * BLK, :] = row

    def own_unit(order):
        dev, slot, store = unit(order)
        transpose_keys(slot)
        fill_mask(dev, jnp.where(slot == 8, 0, slot), True)
        tiles(dev, slot, store, True)

    for cp in loads:
        cp.wait()
    prep(h)
    own_unit(0)
    auxc.wait_recv()
    for cp in xc:
        cp.wait_recv()
    prep(1 - h)
    arrive(other_slot)
    own_unit(1)

    units = jnp.where(first, 9, 4 * x + 1)

    def later(order, _):
        dev, slot, store = unit(order)

        @pl.when(first | (order % 2 == 1))
        def _():
            arrive(slot)
            transpose_keys(slot)

        @pl.when(slot >= 4)
        def _():
            fill_mask(dev, slot, False)
            tiles(dev, slot, store, True)

        pl.when(slot < 4)(lambda: tiles(dev, slot, store, False))
        return 0

    lax.fori_loop(2, units, later, 0)

    def finish(dev):
        tab_c = aux[dev, 0:64, :]
        tab_s = aux[dev, 64:128, :]

        def head(g, _):
            cols = pl.ds(pl.multiple_of(g * D, D), D)
            rows = pl.ds(pl.multiple_of(g * T, T), T)
            inv = 1.0 / esum[dev, g]
            qrt[dev, :, rows] = (qrt[dev, :, rows].astype(F32) * (inv * INV_ROOT)).astype(BF16)
            dot[dev, :, rows] = (dot[dev, :, rows].astype(F32) * inv).astype(BF16)
            up = dqt[dev, g] * (inv * INV_ROOT)
            a, b = up[0:64], up[64:128]
            un = jnp.concatenate([a * tab_c + b * tab_s, b * tab_c - a * tab_s], 0)
            normed = qnt[dev, g]
            qga[...] += un * normed
            gg = un * gain
            dq = qr[dev, g] * (gg - normed * jnp.mean(gg * normed, 0, keepdims=True))
            dqo[dev, :, cols] = nt(eye[...], dq.astype(BF16)).astype(BF16)
            return 0

        lax.fori_loop(0, G, head, 0)

    finish(1 - h)
    dq_far = rcopy(dqo.at[1 - h], dq_hbm.at[:, mine], os_sem, or_sem, partner)
    dq_far.start()
    finish(h)
    dq_near = pltpu.make_async_copy(dqo.at[h], dq_hbm.at[:, mine], lsem.at[0])
    dq_near.start()

    slots = jnp.where(first, 9, 2 * x + 1)

    def partial_copy(slot):
        owner = jnp.where(
            first & (slot < 8), zprev * 8 + 1 + slot, z * 8 + 1 + jnp.where(slot == 8, 0, slot)
        ) % nctx
        place = jnp.where(first & (slot >= 7), 4, x)
        cp = rcopy(
            pbuf.at[slot], red.at[place, h], ps_sem.at[slot], pr_sem.at[place, h], owner
        )
        return owner, place, cp

    def second_pass(slot, _):
        dev = jnp.where(first & (slot < 8), 0, 1)
        store = jnp.where(first, 8 - slot, 2 * (2 * x - slot))
        dkv[0] = nt(gb[store], qrt[dev])
        dkv[1] = nt(eb[store], dot[dev])

        @pl.when(jnp.logical_not(first) & (slot < 2 * x))
        def _():
            dkv[0] += nt(gb[store - 1], qrt[0])
            dkv[1] += nt(eb[store - 1], dot[0])

        pbuf[slot] = dkv[...].astype(BF16)
        owner, place, cp = partial_copy(slot)

        @pl.when(slot == own_slot)
        def _():
            red[place, h] = pbuf[slot]

        pl.when(slot != own_slot)(lambda: cp.start())
        return 0

    lax.fori_loop(0, slots, second_pass, 0)

    own_place = jnp.where(first, 4, x)

    def take(place, head):
        rcopy(
            pbuf.at[0], red.at[place, head], ps_sem.at[0], pr_sem.at[place, head], c
        ).wait_recv()

    take(own_place, 1 - h)
    acc[...] = red[own_place].astype(F32)
    for j in (3, 2, 1, 0):

        @pl.when(source & (True if j == 0 else j > x))
        def _():
            for hh in range(2):
                take(j, hh)
                acc[hh] += red[j, hh].astype(F32)

    kga = jnp.zeros((1, D), F32)
    for hh in range(2):
        dk = acc[hh, 0]
        un = dk * cosn[...] - pltpu.roll(dk, 64, 1) * sinn[...]
        normed = knorm[hh]
        kga += jnp.sum(un * normed, 0, keepdims=True)
        gg = un * kg_ref[...]
        out = krec[hh] * (gg - normed * jnp.mean(gg * normed, -1, keepdims=True))
        dk_ref[:, hh * D : (hh + 1) * D] = out.astype(BF16)
        dv_ref[:, hh * D : (hh + 1) * D] = acc[hh, 1].astype(BF16)

    qcol = jnp.broadcast_to(jnp.sum(qga[...], 1, keepdims=True), (D, D)).T
    sub = lax.broadcasted_iota(jnp.int32, (8, D), 0)
    total = jnp.where(
        sub == 0, qcol[0:8], jnp.where(sub == 1, jnp.broadcast_to(kga, (8, D)), 0.0)
    )
    stages = (
        (ar1, s1, r1, 8, c % 8, lambda n: (z * 8 + (c % 8 + n) % 8, y)),
        (ar2, s2, r2, 4, y, lambda n: (c, (y + n) % 4)),
        (ar3, s3, r3, nz, z, lambda n: ((c + 8 * n) % nctx, y)),
    )
    for buf, ssem, rsem, count, me, peer in stages:
        buf[me] = total
        sends = []
        for n in range(1, count):
            ctx, heads = peer(n)
            sends.append(rcopy(buf.at[me], buf.at[me], ssem.at[n - 1], rsem.at[me], ctx, heads))
        for cp in sends:
            cp.start()
        for n in range(1, count):
            who = (me + n) % count
            rcopy(buf.at[who], buf.at[who], ssem.at[n - 1], rsem.at[who], c).wait_recv()
        total = jnp.sum(buf[...], 0)
        for cp in sends:
            cp.wait_send()
    qgg_ref[...] = total[0:1]
    kgg_ref[...] = total[1:2]

    kv_sends(lambda cp: cp.wait_send())
    kv_on_chip.wait_send()
    auxc.wait_send()
    for cp in xc:
        cp.wait_send()

    def drain(slot, _):
        pl.when(slot != own_slot)(lambda: partial_copy(slot)[2].wait_send())
        return 0

    lax.fori_loop(0, slots, drain, 0)
    dq_near.wait()
    dq_far.wait_send()
    dq_far.wait_recv()


def on_device(nz, q_raw, k_raw, values, saved_out, out_grad, q_gain, k_gain, ancestors):
    lanes = np.arange(D) % (D // 2)
    freq = jnp.asarray(
        np.exp(lanes * (-2.0 * math.log(ROPE_BASE) / D)).astype(np.float32)[None, :]
    )
    vm = pl.BlockSpec(memory_space=pltpu.VMEM)
    hbm = pl.BlockSpec(memory_space=pl.ANY)
    V = pltpu.VMEM
    dma = pltpu.SemaphoreType.DMA
    outs = pl.pallas_call(
        functools.partial(kernel, nz),
        out_shape=(
            jax.ShapeDtypeStruct(q_raw.shape, BF16),
            jax.ShapeDtypeStruct(k_raw.shape, BF16),
            jax.ShapeDtypeStruct(k_raw.shape, BF16),
            jax.ShapeDtypeStruct((1, D), F32),
            jax.ShapeDtypeStruct((1, D), F32),
        ),
        in_specs=[hbm, vm, vm, hbm, hbm, vm, vm, vm, vm],
        out_specs=(hbm, vm, vm, vm, vm),
        scratch_shapes=[
            V((2, T, HALF), BF16), V((2, T, HALF), BF16), V((2, T, HALF), BF16),
            V((9, 2, T, D), BF16), V((2, 2, T, D), BF16), V((9, D, T), BF16),
            V((2, 160, T), F32), V((T, D), F32), V((T, D), F32),
            V((2, T, D), F32), V((2, T, D), F32),
            V((2, D, G * T), BF16), V((2, G, D, T), F32), V((2, G, 1, T), F32),
            V((2, D, G * T), BF16), V((2, G, 1, T), F32), V((2, G, D, T), F32),
            V((2, G, 1, T), F32), V((13, T, G * T), BF16), V((13, T, G * T), BF16),
            V((T, T), F32), V((T, T), BF16), V((2, T, D), F32),
            V((9, 2, T, D), BF16), V((5, 2, 2, T, D), BF16), V((2, T, HALF), BF16),
            V((D, T), F32), V((2, 2, T, D), F32),
            V((8, 8, D), F32), V((4, 8, D), F32), V((nz, 8, D), F32),
            dma((3,)), dma((4,)), dma((4,)), dma((9,)), dma((9,)),
            dma((9,)), dma((5, 2)), dma, dma,
            dma((7,)), dma((8,)), dma((3,)), dma((4,)), dma((nz - 1,)), dma((nz,)),
        ],
        compiler_params=pltpu.CompilerParams(
            collective_id=0, has_side_effects=True, vmem_limit_bytes=63000000
        ),
    )(
        q_raw, k_raw, values, saved_out, out_grad,
        q_gain.reshape(D, 1), k_gain.reshape(1, D), ancestors, freq,
    )
    dq, dk, dv, qg, kg = outs
    return dq, dk, dv, qg.reshape(D), kg.reshape(D)


def solution(mesh):
    nz = mesh.shape["ctx"] // 8
    wide = P("ctx", "heads")
    return jax.shard_map(
        functools.partial(on_device, nz),
        mesh=mesh,
        in_specs=(wide, wide, wide, wide, wide, P(), P(), P("ctx", None)),
        out_specs=(wide, wide, wide, P(), P()),
        check_vma=False,
    )
```

time: 318 us -> 95.6 us (0.30)
  waiting for transfers between devices: 94.1 us -> 0 us
  Pallas kernels: 0 us -> 88.3 us
  blocking collectives: 84 us -> 0 us
  matrix products: 54.6 us -> 0 us
  other arithmetic: 39.4 us -> 0 us
  local copies, waits for them, and re-layouts: 36.9 us -> 6.51 us
  starting transfers between devices: 5.57 us -> 0 us
    ppermute x22 -> x0, waiting for transfers between devices: 94.1 us -> none  [passed_along(): return lax.ppermute(value, axis, pairs)]
    pallas_call x0 -> x1, Pallas kernels: none -> 88.3 us  [on_device(): pl.pallas_call(functools.partial(kernel, nz), out_shape=(jax.ShapeDtypeSt...]
    psum x1 -> x0, blocking collectives: 84 us -> none  [on_device(): lax.psum((q_gain_part, k_gain_part), ('ctx', 'heads'))]
    dot_general x47 -> x0, matrix products: 54.6 us -> none  [the longest x15 15 us: scores_of(): jnp.einsum('ikgd,jkd->kgij', q_rot, key_rot, preferred_element_type=jnp.f...]
    add x31 -> x0, other arithmetic: 16.1 us -> none  [the longest x7 13.4 us: back_step(): grads_now = passed_along(grads_now, 'ctx', 1) + kv_part]
    while x56 -> x0, local copies, waits for them, and re-layouts: 8.61 us -> none
    reduce_sum x9 -> x0, other arithmetic: 7.87 us -> none  [the longest x4 4 us: norm_rope_back(): gain_term = jnp.sum(unrotated * normed, axis=(0, 1))]
    unnamed x68 -> x15, local copies, waits for them, and re-layouts: 13.6 us -> 5.77 us
  transfers between devices with their start and end apart: 22 -> 0, of which waited for: 14 -> 0; matrix products, arithmetic and copies ran while one was open for 22% -> 0% of each run, Pallas kernels for 0% -> 0%
where the time goes in v1:
time: 95.6 us; the launch traced here: 95.5 us
  Pallas kernels  88.3 us (92%)
  local copies, waits for them, and re-layouts  6.51 us (7%)
    pallas_call x1, Pallas kernels, on_device(): pl.pallas_call(functools.partial(kernel, nz), out_shape=(jax.ShapeDtypeSt...  88.3 us
    unnamed x15, local copies, waits for them, and re-layouts  5.77 us

profile of v1, /device:TPU:1, one launch (start us, length us, event | category | flops | bytes accessed | tf_op | source)
XLA Modules:
  0.0 95.5 jit_solution(17553265865398146650)
XLA Ops:
  0.6 0.0 copy-start.2
  0.6 0.6 copy-done.2
  1.3 0.7 copy.14.qg_ref
  2.0 88.3 %shard_map.128 = (bf16[256,2048]{1,0:T(8,128)(2,1)}, bf16[256,256]{1,0:T(8,128)(2,1)}, bf16[256,256]{1,0:T(8,128)(2,1)}, f32[1,128]{1,0:T(1,128)}, f32[1,128]{1,0:T(1,128)}) custom-call(bf16[256,2048]{1,0:T(8,128)(2,1)} %q_hbm.1, bf16[256,256]{1,0:T(8,128)(2,1)} %k_ref.1, bf16[256,256]{1,0:T(8,128)(2,1)} %v_ref.1, bf16[256,2048]{1,0:T(8,128)(2,1)} %so_hbm.1, ...), custom_call_target="tpu_custom_call" | custom-call | tf_op jit(solution)/shard_map/pallas_call | solution.py:426
  90.3 0.0 copy-start.1
  90.4 2.3 %copy.20 = bf16[256,2048]{1,0:T(8,128)(2,1)} copy(bf16[256,2048]{1,0:T(8,128)(2,1)} %get-tuple-element.20) | data formatting | bytes 2097152
  92.7 0.0 copy-done.1
  92.7 0.0 copy-start
  92.7 0.7 copy.21
  93.4 0.3 copy-done
  93.6 0.0 copy-start.4
  93.7 0.7 copy.22
  94.3 0.0 copy-done.4
  94.3 0.0 copy-start.3
  94.3 0.5 copy.23
  94.8 0.1 copy-done.3
  95.0 0.5 copy.24
Async XLA Ops:
  0.6 0.7 copy-start.2
  90.3 2.4 %copy-start.1 = (bf16[256,256]{1,0:T(8,128)(2,1)S(1)}, bf16[256,256]{1,0:T(8,128)(2,1)}, u32[]{:S(2)}) copy-start(bf16[256,256]{1,0:T(8,128)(2,1)} %get-tuple-element.21) | copy-start | bytes 393220
  92.7 1.0 copy-start
  93.6 0.7 copy-start.4
  94.3 0.7 copy-start.3

commit v2 on v1

--- a/solution.py
+++ b/solution.py
@@ -16,6 +16,7 @@
 G = 8
 BLK = 64
 HALF = G * D
+UNROLL = 8
 INV_ROOT = 1.0 / math.sqrt(D)
 EXP_SCALE = INV_ROOT * math.log2(math.e)
 F32 = jnp.float32
@@ -34,9 +35,9 @@
     nz, q_hbm, k_ref, v_ref, so_hbm, do_hbm, qg_ref, kg_ref, anc_ref, fr_ref,
     dq_hbm, dk_ref, dv_ref, qgg_ref, kgg_ref,
     qx, dox, sox, kv, kvs, kt, aux, cosn, sinn, knorm, krec,
-    qrt, qnt, qr, dot, dlt, dqt, esum, eb, gb, mask, eye, dkv, pbuf, red, dqo,
+    qrt, qnt, qr, dot, dlt, dqt, esum, eb, gb, mask, eye, dkv, pbuf, rbuf, red, dqo,
     qga, acc, ar1, ar2, ar3,
-    lsem, xs, xr, kvs_sem, kvr_sem, ps_sem, pr_sem, os_sem, or_sem,
+    lsem, xs, xr, kvs_sem, kvr_sem, ps_sem, pr_sem, rr_sem, fs_sem, os_sem, or_sem,
     s1, r1, s2, r2, s3, r3,
 ):
     c = lax.axis_index("ctx")
@@ -80,13 +81,20 @@
         greet(c, (y + n) % 4)
     for n in range(1, nz):
         greet((c + 8 * n) % nctx)
-    for n in range(2):
-        greet(znext * 8 + n)
-
-    @pl.when(first)
-    def _():
-        for n in range(8):
-            greet(zprev * 8 + n)
+    row = c % 8
+
+    def greet_all(cond, base, places):
+        @pl.when(cond)
+        def _():
+            for n in places:
+                greet(base + n)
+
+    greet_all(first, zprev * 8, range(1, 8))
+    greet_all((row == 1) | (row >= 6), znext * 8, (0, 1))
+    greet_all((row >= 2) & (row <= 5), znext * 8, (2, 3))
+    greetings = (
+        7 + 3 + nz - 1 + jnp.where(first, 3, 0) + jnp.where(x == 1, 4, 0) + jnp.where(row > 0, 2, 0)
+    )
 
     anc = anc_ref[...]
     depth = jnp.sum((anc >= 0).astype(jnp.int32), axis=1, keepdims=True)
@@ -138,51 +146,16 @@
     esum[...] = jnp.zeros_like(esum)
     qga[...] = jnp.zeros_like(qga)
 
-    pl.semaphore_wait(bar, jnp.where(first, 8, 0) + (7 + 3 + nz - 1 + 2))
-
-    kv_on_chip = rcopy(
-        kvs.at[1 - h], kv.at[own_slot], kvs_sem.at[8], kvr_sem.at[own_slot], partner
-    )
-    xc = [
-        rcopy(src.at[:, other], dst.at[h], xs.at[n], xr.at[n], partner)
-        for n, (src, dst) in enumerate(((q_hbm, qx), (do_hbm, dox), (so_hbm, sox)))
-    ]
-    auxc = rcopy(aux.at[h], aux.at[h], xs.at[3], xr.at[3], partner)
-    kv_on_chip.start()
-    auxc.start()
-    for cp in xc:
-        cp.start()
-
-    source = ~(first & (h == 0))
-    position = jnp.where(first, 0, 2 * x - 1 + h)
-
-    def kv_sends(act):
-        for j in range(4):
-            dest = znext * 8 if j == 0 else z * 8 + 2 * j
-            ok = source & (True if j == 0 else j > x)
-
-            @pl.when(ok)
-            def _():
-                for hh in range(2):
-                    act(
-                        rcopy(
-                            kvs.at[hh], kv.at[position], kvs_sem.at[2 * j + hh],
-                            kvr_sem.at[position], dest + hh,
-                        )
-                    )
-
-    kv_sends(lambda cp: cp.start())
-
-    gain = qg_ref[...]
+    gain = jnp.broadcast_to(qg_ref[...], (D, D)).T[:, 0:1]
 
     def prep(dev):
         tab_c = aux[dev, 0:64, :]
         tab_s = aux[dev, 64:128, :]
         ones = jnp.ones((8, D), BF16)
 
-        def head(g, _):
-            cols = pl.ds(pl.multiple_of(g * D, D), D)
-            rows = pl.ds(pl.multiple_of(g * T, T), T)
+        def head(g):
+            cols = slice(g * D, (g + 1) * D)
+            rows = slice(g * T, (g + 1) * T)
             qt = nt(eye[0:D, 0:D], qx[dev, :, cols])
             rec = lax.rsqrt(jnp.mean(qt * qt, 0, keepdims=True) + EPS)
             normed = qt * rec
@@ -199,9 +172,9 @@
             hi = prod.astype(BF16)
             lo = (prod - hi.astype(F32)).astype(BF16)
             dlt[dev, g] = (nt(ones, hi) + nt(ones, lo))[0:1]
-            return 0
-
-        lax.fori_loop(0, G, head, 0)
+
+        for g in range(G):
+            head(g)
 
     def unit(order):
         early = order <= 1
@@ -214,21 +187,27 @@
         rcopy(kvs.at[0], kv.at[slot], kvs_sem.at[0], kvr_sem.at[slot], c).wait_recv()
 
     def tiles(dev, slot, store, masked):
-        def head(g, _):
-            rows = pl.ds(pl.multiple_of(g * T, T), T)
-            st = nn(kv[slot, 0], qrt[dev, :, rows])
-            e = jnp.exp2(st * EXP_SCALE)
-            if masked:
-                e = e * mask[...]
-            esum[dev, g] += jnp.sum(e, 0, keepdims=True)
-            dp = nn(kv[slot, 1], dot[dev, :, rows])
-            gg = (e * (dp - dlt[dev, g])).astype(BF16)
-            eb[store, :, rows] = e.astype(BF16)
-            gb[store, :, rows] = gg
-            dqt[dev, g] += nn(kt[slot], gg)
+        def heads(step, _):
+            keys, vals, keys_t = kv[slot, 0], kv[slot, 1], kt[slot]
+            low = []
+            for u in range(UNROLL):
+                g = step * UNROLL + u
+                rows = pl.ds(pl.multiple_of(g * T, T), T)
+                e = jnp.exp2(nn(keys, qrt[dev, :, rows]) * EXP_SCALE)
+                if masked:
+                    e = e * mask[...]
+                dp = nn(vals, dot[dev, :, rows])
+                gg = (e * (dp - dlt[dev, g])).astype(BF16)
+                low.append((g, rows, e.astype(BF16), gg, jnp.sum(e, 0, keepdims=True)))
+            for g, rows, el, gg, total in low:
+                eb[store, :, rows] = el
+                gb[store, :, rows] = gg
+                esum[dev, g] += total
+            for g, rows, el, gg, total in low:
+                dqt[dev, g] += nn(keys_t, gg)
             return 0
 
-        lax.fori_loop(0, G, head, 0)
+        lax.fori_loop(0, G // UNROLL, heads, 0)
 
     def transpose_keys(slot):
         kt[slot] = nt(eye[0:D, 0:D], kv[slot, 0]).astype(BF16)
@@ -252,6 +231,42 @@
         cp.wait()
     prep(h)
     own_unit(0)
+
+    pl.semaphore_wait(bar, greetings)
+
+    kv_on_chip = rcopy(
+        kvs.at[1 - h], kv.at[own_slot], kvs_sem.at[8], kvr_sem.at[own_slot], partner
+    )
+    xc = [
+        rcopy(src.at[:, other], dst.at[h], xs.at[n], xr.at[n], partner)
+        for n, (src, dst) in enumerate(((q_hbm, qx), (do_hbm, dox), (so_hbm, sox)))
+    ]
+    auxc = rcopy(aux.at[h], aux.at[h], xs.at[3], xr.at[3], partner)
+    kv_on_chip.start()
+    auxc.start()
+    for cp in xc:
+        cp.start()
+
+    source = ~(first & (h == 0))
+    position = jnp.where(first, 0, 2 * x - 1 + h)
+
+    def kv_sends(act):
+        for j in range(4):
+            dest = znext * 8 if j == 0 else z * 8 + 2 * j
+            ok = source & (True if j == 0 else j > x)
+
+            @pl.when(ok)
+            def _():
+                for hh in range(2):
+                    act(
+                        rcopy(
+                            kvs.at[hh], kv.at[position], kvs_sem.at[2 * j + hh],
+                            kvr_sem.at[position], dest + hh,
+                        )
+                    )
+
+    kv_sends(lambda cp: cp.start())
+
     auxc.wait_recv()
     for cp in xc:
         cp.wait_recv()
@@ -282,31 +297,28 @@
     def finish(dev):
         tab_c = aux[dev, 0:64, :]
         tab_s = aux[dev, 64:128, :]
-
-        def head(g, _):
-            cols = pl.ds(pl.multiple_of(g * D, D), D)
-            rows = pl.ds(pl.multiple_of(g * T, T), T)
-            inv = 1.0 / esum[dev, g]
-            qrt[dev, :, rows] = (qrt[dev, :, rows].astype(F32) * (inv * INV_ROOT)).astype(BF16)
-            dot[dev, :, rows] = (dot[dev, :, rows].astype(F32) * inv).astype(BF16)
-            up = dqt[dev, g] * (inv * INV_ROOT)
+        part = jnp.zeros((D, T), F32)
+        for g in range(G):
+            up = dqt[dev, g] * (esum[dev, g] * INV_ROOT)
             a, b = up[0:64], up[64:128]
             un = jnp.concatenate([a * tab_c + b * tab_s, b * tab_c - a * tab_s], 0)
             normed = qnt[dev, g]
-            qga[...] += un * normed
+            part += un * normed
             gg = un * gain
             dq = qr[dev, g] * (gg - normed * jnp.mean(gg * normed, 0, keepdims=True))
-            dqo[dev, :, cols] = nt(eye[...], dq.astype(BF16)).astype(BF16)
-            return 0
-
-        lax.fori_loop(0, G, head, 0)
-
-    finish(1 - h)
-    dq_far = rcopy(dqo.at[1 - h], dq_hbm.at[:, mine], os_sem, or_sem, partner)
-    dq_far.start()
-    finish(h)
-    dq_near = pltpu.make_async_copy(dqo.at[h], dq_hbm.at[:, mine], lsem.at[0])
-    dq_near.start()
+            dqo[dev, :, g * D : (g + 1) * D] = nt(eye[...], dq.astype(BF16)).astype(BF16)
+        qga[...] += part
+
+    def normalise(dev):
+        for g in range(G):
+            rows = slice(g * T, (g + 1) * T)
+            inv = 1.0 / esum[dev, g]
+            esum[dev, g] = inv
+            qrt[dev, :, rows] = (qrt[dev, :, rows].astype(F32) * (inv * INV_ROOT)).astype(BF16)
+            dot[dev, :, rows] = (dot[dev, :, rows].astype(F32) * inv).astype(BF16)
+
+    for dev in range(2):
+        normalise(dev)
 
     slots = jnp.where(first, 9, 2 * x + 1)
 
@@ -338,10 +350,37 @@
         def _():
             red[place, h] = pbuf[slot]
 
-        pl.when(slot != own_slot)(lambda: cp.start())
+        far = first & (slot >= 1) & (slot <= 4)
+        pl.when((slot != own_slot) & jnp.logical_not(far))(lambda: cp.start())
+
+        @pl.when(far)
+        def _():
+            place = jnp.clip(slot - 1, 0, 3)
+            rcopy(
+                pbuf.at[slot], rbuf.at[place], ps_sem.at[slot], rr_sem.at[place], z * 8 + 2 + h
+            ).start()
+
         return 0
 
     lax.fori_loop(0, slots, second_pass, 0)
+
+    finish(1 - h)
+    dq_far = rcopy(dqo.at[1 - h], dq_hbm.at[:, mine], os_sem, or_sem, partner)
+    dq_far.start()
+    finish(h)
+    dq_near = pltpu.make_async_copy(dqo.at[h], dq_hbm.at[:, mine], lsem.at[0])
+    dq_near.start()
+
+    def passing(n):
+        return rcopy(
+            rbuf.at[n], red.at[0, h], fs_sem.at[n], pr_sem.at[0, h], zprev * 8 + 2 + n
+        )
+
+    @pl.when(x == 1)
+    def _():
+        for n in range(4):
+            rcopy(pbuf.at[0], rbuf.at[n], ps_sem.at[0], rr_sem.at[n], c).wait_recv()
+            passing(n).start()
 
     own_place = jnp.where(first, 4, x)
 
@@ -409,9 +448,33 @@
         return 0
 
     lax.fori_loop(0, slots, drain, 0)
+
+    @pl.when(x == 1)
+    def _():
+        for n in range(4):
+            passing(n).wait_send()
+
     dq_near.wait()
     dq_far.wait_send()
     dq_far.wait_recv()
+
+
+def emit(dq, dk, dv, qg, kg, dq_out, dk_out, dv_out, qg_out, kg_out, big, small, isem, osem):
+    pieces = [(dk, small.at[0], dk_out), (dv, small.at[1], dv_out)]
+    for n in range(4):
+        rows = pl.ds(n * 64, 64)
+        pieces.append((dq.at[rows], big.at[rows], dq_out.at[rows]))
+    ins = [pltpu.make_async_copy(a, b, isem.at[n]) for n, (a, b, _) in enumerate(pieces)]
+    outs = [pltpu.make_async_copy(b, o, osem.at[n]) for n, (_, b, o) in enumerate(pieces)]
+    for cp in ins:
+        cp.start()
+    qg_out[...] = qg[0]
+    kg_out[...] = kg[0]
+    for a, b in zip(ins, outs):
+        a.wait()
+        b.start()
+    for b in outs:
+        b.wait()
 
 
 def on_device(nz, q_raw, k_raw, values, saved_out, out_grad, q_gain, k_gain, ancestors):
@@ -443,11 +506,11 @@
             V((2, D, G * T), BF16), V((2, G, 1, T), F32), V((2, G, D, T), F32),
             V((2, G, 1, T), F32), V((13, T, G * T), BF16), V((13, T, G * T), BF16),
             V((T, T), F32), V((T, T), BF16), V((2, T, D), F32),
-            V((9, 2, T, D), BF16), V((5, 2, 2, T, D), BF16), V((2, T, HALF), BF16),
+            V((9, 2, T, D), BF16), V((4, 2, T, D), BF16), V((5, 2, 2, T, D), BF16), V((2, T, HALF), BF16),
             V((D, T), F32), V((2, 2, T, D), F32),
             V((8, 8, D), F32), V((4, 8, D), F32), V((nz, 8, D), F32),
             dma((3,)), dma((4,)), dma((4,)), dma((9,)), dma((9,)),
-            dma((9,)), dma((5, 2)), dma, dma,
+            dma((9,)), dma((5, 2)), dma((4,)), dma((4,)), dma, dma,
             dma((7,)), dma((8,)), dma((3,)), dma((4,)), dma((nz - 1,)), dma((nz,)),
         ],
         compiler_params=pltpu.CompilerParams(
@@ -455,10 +518,23 @@
         ),
     )(
         q_raw, k_raw, values, saved_out, out_grad,
-        q_gain.reshape(D, 1), k_gain.reshape(1, D), ancestors, freq,
-    )
-    dq, dk, dv, qg, kg = outs
-    return dq, dk, dv, qg.reshape(D), kg.reshape(D)
+        q_gain.reshape(1, D), k_gain.reshape(1, D), ancestors, freq,
+    )
+    return pl.pallas_call(
+        emit,
+        out_shape=(
+            jax.ShapeDtypeStruct(q_raw.shape, BF16),
+            jax.ShapeDtypeStruct(k_raw.shape, BF16),
+            jax.ShapeDtypeStruct(k_raw.shape, BF16),
+            jax.ShapeDtypeStruct((D,), F32),
+            jax.ShapeDtypeStruct((D,), F32),
+        ),
+        in_specs=[hbm, hbm, hbm, vm, vm],
+        out_specs=(hbm, hbm, hbm, vm, vm),
+        scratch_shapes=[
+            V(q_raw.shape, BF16), V((2,) + k_raw.shape, BF16), dma((6,)), dma((6,)),
+        ],
+    )(*outs)
 
 
 def solution(mesh):

time: 95.6 us -> 65.2 us (0.68)
  Pallas kernels: 88.3 us -> 64.4 us
  local copies, waits for them, and re-layouts: 6.51 us -> 0 us
    pallas_call x1, Pallas kernels: 88.3 us -> 61 us  [on_device(): pl.pallas_call(functools.partial(kernel, nz), out_shape=(jax.ShapeDtypeSt...]
    unnamed x15 -> x0, local copies, waits for them, and re-layouts: 5.77 us -> none
    pallas_call x0 -> x1, Pallas kernels: none -> 3.33 us  [on_device(): pl.pallas_call(emit, out_shape=(jax.ShapeDtypeStruct(q_raw.shape, BF16),...]
where the time goes in v2:
time: 65.2 us; the launch traced here: 65 us
  Pallas kernels  64.4 us (99%)
    pallas_call x1, Pallas kernels, on_device(): pl.pallas_call(functools.partial(kernel, nz), out_shape=(jax.ShapeDtypeSt...  61 us
    pallas_call x1, Pallas kernels, on_device(): pl.pallas_call(emit, out_shape=(jax.ShapeDtypeStruct(q_raw.shape, BF16),...  3.33 us

profile of v2, /device:TPU:1, one launch (start us, length us, event | category | flops | bytes accessed | tf_op | source)
XLA Modules:
  0.0 65.0 jit_solution(10207514798533700813)
XLA Ops:
  0.6 61.0 %shard_map.128 = (bf16[256,2048]{1,0:T(8,128)(2,1)}, bf16[256,256]{1,0:T(8,128)(2,1)}, bf16[256,256]{1,0:T(8,128)(2,1)}, f32[1,128]{1,0:T(1,128)}, f32[1,128]{1,0:T(1,128)}) custom-call(bf16[256,2048]{1,0:T(8,128)(2,1)} %q_hbm.1, bf16[256,256]{1,0:T(8,128)(2,1)} %k_ref.1, bf16[256,256]{1,0:T(8,128)(2,1)} %v_ref.1, bf16[256,2048]{1,0:T(8,128)(2,1)} %so_hbm.1, ...), custom_call_target="tpu_custom_call" | custom-call | tf_op jit(solution)/shard_map/pallas_call | solution.py:489
  61.7 3.3 %shard_map.129 = (bf16[256,2048]{1,0:T(8,128)(2,1)}, bf16[256,256]{1,0:T(8,128)(2,1)}, bf16[256,256]{1,0:T(8,128)(2,1)}, f32[128]{0:T(128)}, f32[128]{0:T(128)}) custom-call(bf16[256,2048]{1,0:T(8,128)(2,1)} %get-tuple-element.10.dq, bf16[256,256]{1,0:T(8,128)(2,1)} %get-tuple-element.11.dk, bf16[256,256]{1,0:T(8,128)(2,1)} %get-tuple-element.12.dv, ...), custom_call_target="tpu_custom_call" | custom-call | tf_op jit(solution)/shard_map/pallas_call | solution.py:523

commit v3 on v2

--- a/solution.py
+++ b/solution.py
@@ -36,7 +36,7 @@
     dq_hbm, dk_ref, dv_ref, qgg_ref, kgg_ref,
     qx, dox, sox, kv, kvs, kt, aux, cosn, sinn, knorm, krec,
     qrt, qnt, qr, dot, dlt, dqt, esum, eb, gb, mask, eye, dkv, pbuf, rbuf, red, dqo,
-    qga, acc, ar1, ar2, ar3,
+    qga, kga, toff, tblk, acc, ar1, ar2, ar3,
     lsem, xs, xr, kvs_sem, kvr_sem, ps_sem, pr_sem, rr_sem, fs_sem, os_sem, or_sem,
     s1, r1, s2, r2, s3, r3,
 ):
@@ -145,6 +145,11 @@
     dqt[...] = jnp.zeros_like(dqt)
     esum[...] = jnp.zeros_like(esum)
     qga[...] = jnp.zeros_like(qga)
+    kga[...] = jnp.zeros_like(kga)
+    sign = jnp.where(lane[0:1] < 64, -1.0, 1.0)
+    ang_off = off.astype(F32) * fr_ref[...]
+    toff[0] = jnp.cos(ang_off)
+    toff[1] = jnp.sin(ang_off) * sign
 
     gain = jnp.broadcast_to(qg_ref[...], (D, D)).T[:, 0:1]
 
@@ -274,6 +279,19 @@
     arrive(other_slot)
     own_unit(1)
 
+    tri = jnp.where(
+        lax.broadcasted_iota(jnp.int32, (32, 32), 0) >= lax.broadcasted_iota(jnp.int32, (32, 32), 1),
+        1.0, 0.0,
+    ).astype(BF16)
+    count = jnp.ones((32, 1), F32)
+    for dev in range(2):
+        seen = aux[dev, 128:160, :]
+        upto = nn(tri, seen.astype(BF16))
+        count = jnp.maximum(count, jnp.max(seen * upto, axis=1, keepdims=True))
+    ang_blk = jnp.broadcast_to((count - 1.0) * BLK, (32, D)) * fr_ref[...]
+    tblk[0] = jnp.cos(ang_blk)
+    tblk[1] = jnp.sin(ang_blk) * sign
+
     units = jnp.where(first, 9, 4 * x + 1)
 
     def later(order, _):
@@ -344,6 +362,21 @@
             dkv[1] += nt(eb[store - 1], dot[0])
 
         pbuf[slot] = dkv[...].astype(BF16)
+        gains = jnp.zeros((1, D), F32)
+        for j in range(4):
+            place = pl.ds(4 * jnp.where(slot == 8, 0, slot) + j, 1)
+            part = slice(j * BLK, (j + 1) * BLK)
+            cos_b, sin_b = tblk[0, place, :], tblk[1, place, :]
+            cos_k = cos_b * toff[0] - sin_b * toff[1]
+            sin_k = sin_b * toff[0] + cos_b * toff[1]
+            dkp = dkv[0, part]
+            key = kv[slot, 0, part].astype(F32)
+            gains += jnp.sum(
+                (dkp * cos_k - pltpu.roll(dkp, 64, 1) * sin_k)
+                * (key * cos_k - pltpu.roll(key, 64, 1) * sin_k),
+                0, keepdims=True,
+            )
+        kga[...] += gains
         owner, place, cp = partial_copy(slot)
 
         @pl.when(slot == own_slot)
@@ -371,56 +404,18 @@
     dq_near = pltpu.make_async_copy(dqo.at[h], dq_hbm.at[:, mine], lsem.at[0])
     dq_near.start()
 
-    def passing(n):
-        return rcopy(
-            rbuf.at[n], red.at[0, h], fs_sem.at[n], pr_sem.at[0, h], zprev * 8 + 2 + n
-        )
-
-    @pl.when(x == 1)
-    def _():
-        for n in range(4):
-            rcopy(pbuf.at[0], rbuf.at[n], ps_sem.at[0], rr_sem.at[n], c).wait_recv()
-            passing(n).start()
-
-    own_place = jnp.where(first, 4, x)
-
-    def take(place, head):
-        rcopy(
-            pbuf.at[0], red.at[place, head], ps_sem.at[0], pr_sem.at[place, head], c
-        ).wait_recv()
-
-    take(own_place, 1 - h)
-    acc[...] = red[own_place].astype(F32)
-    for j in (3, 2, 1, 0):
-
-        @pl.when(source & (True if j == 0 else j > x))
-        def _():
-            for hh in range(2):
-                take(j, hh)
-                acc[hh] += red[j, hh].astype(F32)
-
-    kga = jnp.zeros((1, D), F32)
-    for hh in range(2):
-        dk = acc[hh, 0]
-        un = dk * cosn[...] - pltpu.roll(dk, 64, 1) * sinn[...]
-        normed = knorm[hh]
-        kga += jnp.sum(un * normed, 0, keepdims=True)
-        gg = un * kg_ref[...]
-        out = krec[hh] * (gg - normed * jnp.mean(gg * normed, -1, keepdims=True))
-        dk_ref[:, hh * D : (hh + 1) * D] = out.astype(BF16)
-        dv_ref[:, hh * D : (hh + 1) * D] = acc[hh, 1].astype(BF16)
-
     qcol = jnp.broadcast_to(jnp.sum(qga[...], 1, keepdims=True), (D, D)).T
     sub = lax.broadcasted_iota(jnp.int32, (8, D), 0)
-    total = jnp.where(
-        sub == 0, qcol[0:8], jnp.where(sub == 1, jnp.broadcast_to(kga, (8, D)), 0.0)
-    )
+    ksum = jnp.broadcast_to(kga[...] / kg_ref[...], (8, D))
+    total = jnp.where(sub == 0, qcol[0:8], jnp.where(sub == 1, ksum, 0.0))
     stages = (
         (ar1, s1, r1, 8, c % 8, lambda n: (z * 8 + (c % 8 + n) % 8, y)),
         (ar2, s2, r2, 4, y, lambda n: (c, (y + n) % 4)),
         (ar3, s3, r3, nz, z, lambda n: ((c + 8 * n) % nctx, y)),
     )
-    for buf, ssem, rsem, count, me, peer in stages:
+
+    def give(stage, total):
+        buf, ssem, rsem, count, me, peer = stage
         buf[me] = total
         sends = []
         for n in range(1, count):
@@ -428,14 +423,65 @@
             sends.append(rcopy(buf.at[me], buf.at[me], ssem.at[n - 1], rsem.at[me], ctx, heads))
         for cp in sends:
             cp.start()
+        return sends
+
+    def collect(stage):
+        buf, ssem, rsem, count, me, peer = stage
         for n in range(1, count):
             who = (me + n) % count
             rcopy(buf.at[who], buf.at[who], ssem.at[n - 1], rsem.at[who], c).wait_recv()
-        total = jnp.sum(buf[...], 0)
-        for cp in sends:
-            cp.wait_send()
+        return jnp.sum(buf[...], 0)
+
+    given = give(stages[0], total)
+    def passing(n):
+        return rcopy(
+            rbuf.at[n], red.at[0, h], fs_sem.at[n], pr_sem.at[0, h], zprev * 8 + 2 + n
+        )
+
+    def relay(places):
+        @pl.when(x == 1)
+        def _():
+            for n in places:
+                rcopy(pbuf.at[0], rbuf.at[n], ps_sem.at[0], rr_sem.at[n], c).wait_recv()
+                passing(n).start()
+
+    relay((0, 1))
+    given += give(stages[1], collect(stages[0]))
+    relay((2,))
+    given += give(stages[2], collect(stages[1]))
+    relay((3,))
+
+    own_place = jnp.where(first, 4, x)
+
+    def take(place, head):
+        rcopy(
+            pbuf.at[0], red.at[place, head], ps_sem.at[0], pr_sem.at[place, head], c
+        ).wait_recv()
+
+    take(own_place, 1 - h)
+    acc[...] = red[own_place].astype(F32)
+    for j in (3, 2, 1, 0):
+
+        @pl.when(source & (True if j == 0 else j > x))
+        def _():
+            for hh in range(2):
+                take(j, hh)
+                acc[hh] += red[j, hh].astype(F32)
+
+    for hh in range(2):
+        dk = acc[hh, 0]
+        un = dk * cosn[...] - pltpu.roll(dk, 64, 1) * sinn[...]
+        normed = knorm[hh]
+        gg = un * kg_ref[...]
+        out = krec[hh] * (gg - normed * jnp.mean(gg * normed, -1, keepdims=True))
+        dk_ref[:, hh * D : (hh + 1) * D] = out.astype(BF16)
+        dv_ref[:, hh * D : (hh + 1) * D] = acc[hh, 1].astype(BF16)
+
+    total = collect(stages[2])
     qgg_ref[...] = total[0:1]
     kgg_ref[...] = total[1:2]
+    for cp in given:
+        cp.wait_send()
 
     kv_sends(lambda cp: cp.wait_send())
     kv_on_chip.wait_send()
@@ -507,7 +553,8 @@
             V((2, G, 1, T), F32), V((13, T, G * T), BF16), V((13, T, G * T), BF16),
             V((T, T), F32), V((T, T), BF16), V((2, T, D), F32),
             V((9, 2, T, D), BF16), V((4, 2, T, D), BF16), V((5, 2, 2, T, D), BF16), V((2, T, HALF), BF16),
-            V((D, T), F32), V((2, 2, T, D), F32),
+            V((D, T), F32), V((1, D), F32), V((2, BLK, D), F32), V((2, 32, D), F32),
+            V((2, 2, T, D), F32),
             V((8, 8, D), F32), V((4, 8, D), F32), V((nz, 8, D), F32),
             dma((3,)), dma((4,)), dma((4,)), dma((9,)), dma((9,)),
             dma((9,)), dma((5, 2)), dma((4,)), dma((4,)), dma, dma,

time: 65.2 us -> 60.9 us (0.934)
  Pallas kernels: 64.4 us -> 59.8 us
    pallas_call x1, Pallas kernels: 61 us -> 56.4 us  [on_device(): pl.pallas_call(functools.partial(kernel, nz), out_shape=(jax.ShapeDtypeSt...]
where the time goes in v3:
time: 60.9 us; the launch traced here: 60.4 us
  Pallas kernels  59.8 us (98%)
  between operations  0.64 us (1%)
    pallas_call x1, Pallas kernels, on_device(): pl.pallas_call(functools.partial(kernel, nz), out_shape=(jax.ShapeDtypeSt...  56.4 us
    pallas_call x1, Pallas kernels, on_device(): pl.pallas_call(emit, out_shape=(jax.ShapeDtypeStruct(q_raw.shape, BF16),...  3.33 us

profile of v3, /device:TPU:1, one launch (start us, length us, event | category | flops | bytes accessed | tf_op | source)
XLA Modules:
  0.0 60.4 jit_solution(5318708962479347053)
XLA Ops:
  0.6 56.4 %shard_map.128 = (bf16[256,2048]{1,0:T(8,128)(2,1)}, bf16[256,256]{1,0:T(8,128)(2,1)}, bf16[256,256]{1,0:T(8,128)(2,1)}, f32[1,128]{1,0:T(1,128)}, f32[1,128]{1,0:T(1,128)}) custom-call(bf16[256,2048]{1,0:T(8,128)(2,1)} %q_hbm.1, bf16[256,256]{1,0:T(8,128)(2,1)} %k_ref.1, bf16[256,256]{1,0:T(8,128)(2,1)} %v_ref.1, bf16[256,2048]{1,0:T(8,128)(2,1)} %so_hbm.1, ...), custom_call_target="tpu_custom_call" | custom-call | tf_op jit(solution)/shard_map/pallas_call | solution.py:535
  57.1 3.3 %shard_map.129 = (bf16[256,2048]{1,0:T(8,128)(2,1)}, bf16[256,256]{1,0:T(8,128)(2,1)}, bf16[256,256]{1,0:T(8,128)(2,1)}, f32[128]{0:T(128)}, f32[128]{0:T(128)}) custom-call(bf16[256,2048]{1,0:T(8,128)(2,1)} %get-tuple-element.10.dq, bf16[256,256]{1,0:T(8,128)(2,1)} %get-tuple-element.11.dk, bf16[256,256]{1,0:T(8,128)(2,1)} %get-tuple-element.12.dv, ...), custom_call_target="tpu_custom_call" | custom-call | tf_op jit(solution)/shard_map/pallas_call | solution.py:570

commit v4 on v3

--- a/solution.py
+++ b/solution.py
@@ -35,7 +35,7 @@
     nz, q_hbm, k_ref, v_ref, so_hbm, do_hbm, qg_ref, kg_ref, anc_ref, fr_ref,
     dq_hbm, dk_ref, dv_ref, qgg_ref, kgg_ref,
     qx, dox, sox, kv, kvs, kt, aux, cosn, sinn, knorm, krec,
-    qrt, qnt, qr, dot, dlt, dqt, esum, eb, gb, mask, eye, dkv, pbuf, rbuf, red, dqo,
+    qrt, qnt, qr, dot, dos, dlt, dqt, esum, eb, gb, mask, eye, dkv, pbuf, rbuf, red, dqo,
     qga, kga, toff, tblk, acc, ar1, ar2, ar3,
     lsem, xs, xr, kvs_sem, kvr_sem, ps_sem, pr_sem, rr_sem, fs_sem, os_sem, or_sem,
     s1, r1, s2, r2, s3, r3,
@@ -188,27 +188,39 @@
         dev = jnp.where(first, jnp.where(swapped == 0, 1, 0), 1 - swapped % 2)
         return dev, slot, swapped
 
-    def arrive(slot):
-        rcopy(kvs.at[0], kv.at[slot], kvs_sem.at[0], kvr_sem.at[slot], c).wait_recv()
+    def arrive(slot, n):
+        rcopy(
+            kvs.at[0, n], kv.at[slot, n], kvs_sem.at[n, 0], kvr_sem.at[n, slot], c
+        ).wait_recv()
 
     def tiles(dev, slot, store, masked):
         def heads(step, _):
-            keys, vals, keys_t = kv[slot, 0], kv[slot, 1], kt[slot]
-            low = []
+            keys = kv[slot, 0]
             for u in range(UNROLL):
                 g = step * UNROLL + u
                 rows = pl.ds(pl.multiple_of(g * T, T), T)
                 e = jnp.exp2(nn(keys, qrt[dev, :, rows]) * EXP_SCALE)
                 if masked:
                     e = e * mask[...]
+                eb[store, :, rows] = e.astype(BF16)
+                esum[dev, g] += jnp.sum(e, 0, keepdims=True)
+            return 0
+
+        lax.fori_loop(0, G // UNROLL, heads, 0)
+
+    def grad_tiles(dev, slot, store):
+        def heads(step, _):
+            vals, keys_t = kv[slot, 1], kt[slot]
+            low = []
+            for u in range(UNROLL):
+                g = step * UNROLL + u
+                rows = pl.ds(pl.multiple_of(g * T, T), T)
                 dp = nn(vals, dot[dev, :, rows])
-                gg = (e * (dp - dlt[dev, g])).astype(BF16)
-                low.append((g, rows, e.astype(BF16), gg, jnp.sum(e, 0, keepdims=True)))
-            for g, rows, el, gg, total in low:
-                eb[store, :, rows] = el
+                gg = (eb[store, :, rows].astype(F32) * (dp - dlt[dev, g])).astype(BF16)
+                low.append((g, rows, gg))
+            for g, rows, gg in low:
                 gb[store, :, rows] = gg
-                esum[dev, g] += total
-            for g, rows, el, gg, total in low:
+            for g, rows, gg in low:
                 dqt[dev, g] += nn(keys_t, gg)
             return 0
 
@@ -239,15 +251,18 @@
 
     pl.semaphore_wait(bar, greetings)
 
-    kv_on_chip = rcopy(
-        kvs.at[1 - h], kv.at[own_slot], kvs_sem.at[8], kvr_sem.at[own_slot], partner
-    )
+    kv_on_chip = [
+        rcopy(
+            kvs.at[1 - h, n], kv.at[own_slot, n], kvs_sem.at[n, 8], kvr_sem.at[n, own_slot], partner
+        )
+        for n in range(2)
+    ]
     xc = [
         rcopy(src.at[:, other], dst.at[h], xs.at[n], xr.at[n], partner)
         for n, (src, dst) in enumerate(((q_hbm, qx), (do_hbm, dox), (so_hbm, sox)))
     ]
     auxc = rcopy(aux.at[h], aux.at[h], xs.at[3], xr.at[3], partner)
-    kv_on_chip.start()
+    kv_on_chip[0].start()
     auxc.start()
     for cp in xc:
         cp.start()
@@ -256,27 +271,29 @@
     position = jnp.where(first, 0, 2 * x - 1 + h)
 
     def kv_sends(act):
-        for j in range(4):
-            dest = znext * 8 if j == 0 else z * 8 + 2 * j
-            ok = source & (True if j == 0 else j > x)
-
-            @pl.when(ok)
-            def _():
-                for hh in range(2):
-                    act(
-                        rcopy(
-                            kvs.at[hh], kv.at[position], kvs_sem.at[2 * j + hh],
-                            kvr_sem.at[position], dest + hh,
+        for n in range(2):
+            for j in range(4):
+                dest = znext * 8 if j == 0 else z * 8 + 2 * j
+                ok = source & (True if j == 0 else j > x)
+
+                @pl.when(ok)
+                def _():
+                    for hh in range(2):
+                        act(
+                            rcopy(
+                                kvs.at[hh, n], kv.at[position, n], kvs_sem.at[n, 2 * j + hh],
+                                kvr_sem.at[n, position], dest + hh,
+                            )
                         )
-                    )
 
     kv_sends(lambda cp: cp.start())
+    kv_on_chip[1].start()
 
     auxc.wait_recv()
     for cp in xc:
         cp.wait_recv()
     prep(1 - h)
-    arrive(other_slot)
+    arrive(other_slot, 0)
     own_unit(1)
 
     tri = jnp.where(
@@ -299,7 +316,7 @@
 
         @pl.when(first | (order % 2 == 1))
         def _():
-            arrive(slot)
+            arrive(slot, 0)
             transpose_keys(slot)
 
         @pl.when(slot >= 4)
@@ -333,7 +350,7 @@
             inv = 1.0 / esum[dev, g]
             esum[dev, g] = inv
             qrt[dev, :, rows] = (qrt[dev, :, rows].astype(F32) * (inv * INV_ROOT)).astype(BF16)
-            dot[dev, :, rows] = (dot[dev, :, rows].astype(F32) * inv).astype(BF16)
+            dos[dev, :, rows] = (dot[dev, :, rows].astype(F32) * inv).astype(BF16)
 
     for dev in range(2):
         normalise(dev)
@@ -350,16 +367,20 @@
         )
         return owner, place, cp
 
-    def second_pass(slot, _):
+    def second_pass(step, _):
+        slot = step
         dev = jnp.where(first & (slot < 8), 0, 1)
         store = jnp.where(first, 8 - slot, 2 * (2 * x - slot))
+        pl.when(slot != own_slot)(lambda: arrive(slot, 1))
+        grad_tiles(dev, slot, store)
         dkv[0] = nt(gb[store], qrt[dev])
-        dkv[1] = nt(eb[store], dot[dev])
+        dkv[1] = nt(eb[store], dos[dev])
 
         @pl.when(jnp.logical_not(first) & (slot < 2 * x))
         def _():
+            grad_tiles(0, slot, store - 1)
             dkv[0] += nt(gb[store - 1], qrt[0])
-            dkv[1] += nt(eb[store - 1], dot[0])
+            dkv[1] += nt(eb[store - 1], dos[0])
 
         pbuf[slot] = dkv[...].astype(BF16)
         gains = jnp.zeros((1, D), F32)
@@ -484,7 +505,8 @@
         cp.wait_send()
 
     kv_sends(lambda cp: cp.wait_send())
-    kv_on_chip.wait_send()
+    for cp in kv_on_chip:
+        cp.wait_send()
     auxc.wait_send()
     for cp in xc:
         cp.wait_send()
@@ -549,14 +571,14 @@
             V((2, 160, T), F32), V((T, D), F32), V((T, D), F32),
             V((2, T, D), F32), V((2, T, D), F32),
             V((2, D, G * T), BF16), V((2, G, D, T), F32), V((2, G, 1, T), F32),
-            V((2, D, G * T), BF16), V((2, G, 1, T), F32), V((2, G, D, T), F32),
+            V((2, D, G * T), BF16), V((2, D, G * T), BF16), V((2, G, 1, T), F32), V((2, G, D, T), F32),
             V((2, G, 1, T), F32), V((13, T, G * T), BF16), V((13, T, G * T), BF16),
             V((T, T), F32), V((T, T), BF16), V((2, T, D), F32),
             V((9, 2, T, D), BF16), V((4, 2, T, D), BF16), V((5, 2, 2, T, D), BF16), V((2, T, HALF), BF16),
             V((D, T), F32), V((1, D), F32), V((2, BLK, D), F32), V((2, 32, D), F32),
             V((2, 2, T, D), F32),
             V((8, 8, D), F32), V((4, 8, D), F32), V((nz, 8, D), F32),
-            dma((3,)), dma((4,)), dma((4,)), dma((9,)), dma((9,)),
+            dma((3,)), dma((4,)), dma((4,)), dma((2, 9)), dma((2, 9)),
             dma((9,)), dma((5, 2)), dma((4,)), dma((4,)), dma, dma,
             dma((7,)), dma((8,)), dma((3,)), dma((4,)), dma((nz - 1,)), dma((nz,)),
         ],

time: 60.9 us -> 58.8 us (0.966)
  Pallas kernels: 59.8 us -> 57.4 us
    pallas_call x1, Pallas kernels: 56.4 us -> 54 us  [on_device(): pl.pallas_call(functools.partial(kernel, nz), out_shape=(jax.ShapeDtypeSt...]
where the time goes in v4:
time: 58.8 us; the launch traced here: 58 us
  Pallas kernels  57.4 us (98%)
  between operations  0.64 us (1%)
    pallas_call x1, Pallas kernels, on_device(): pl.pallas_call(functools.partial(kernel, nz), out_shape=(jax.ShapeDtypeSt...  54 us
    pallas_call x1, Pallas kernels, on_device(): pl.pallas_call(emit, out_shape=(jax.ShapeDtypeStruct(q_raw.shape, BF16),...  3.33 us

profile of v4, /device:TPU:1, one launch (start us, length us, event | category | flops | bytes accessed | tf_op | source)
XLA Modules:
  0.0 58.0 jit_solution(9835058057042417911)
XLA Ops:
  0.6 54.0 %shard_map.128 = (bf16[256,2048]{1,0:T(8,128)(2,1)}, bf16[256,256]{1,0:T(8,128)(2,1)}, bf16[256,256]{1,0:T(8,128)(2,1)}, f32[1,128]{1,0:T(1,128)}, f32[1,128]{1,0:T(1,128)}) custom-call(bf16[256,2048]{1,0:T(8,128)(2,1)} %q_hbm.1, bf16[256,256]{1,0:T(8,128)(2,1)} %k_ref.1, bf16[256,256]{1,0:T(8,128)(2,1)} %v_ref.1, bf16[256,2048]{1,0:T(8,128)(2,1)} %so_hbm.1, ...), custom_call_target="tpu_custom_call" | custom-call | tf_op jit(solution)/shard_map/pallas_call | solution.py:557
  54.7 3.3 %shard_map.129 = (bf16[256,2048]{1,0:T(8,128)(2,1)}, bf16[256,256]{1,0:T(8,128)(2,1)}, bf16[256,256]{1,0:T(8,128)(2,1)}, f32[128]{0:T(128)}, f32[128]{0:T(128)}) custom-call(bf16[256,2048]{1,0:T(8,128)(2,1)} %get-tuple-element.10.dq, bf16[256,256]{1,0:T(8,128)(2,1)} %get-tuple-element.11.dk, bf16[256,256]{1,0:T(8,128)(2,1)} %get-tuple-element.12.dv, ...), custom_call_target="tpu_custom_call" | custom-call | tf_op jit(solution)/shard_map/pallas_call | solution.py:592

commit v5 on v4

--- a/solution.py
+++ b/solution.py
@@ -357,15 +357,33 @@
 
     slots = jnp.where(first, 9, 2 * x + 1)
 
-    def partial_copy(slot):
+    def partial_copy(slot, n):
         owner = jnp.where(
             first & (slot < 8), zprev * 8 + 1 + slot, z * 8 + 1 + jnp.where(slot == 8, 0, slot)
         ) % nctx
         place = jnp.where(first & (slot >= 7), 4, x)
         cp = rcopy(
-            pbuf.at[slot], red.at[place, h], ps_sem.at[slot], pr_sem.at[place, h], owner
+            pbuf.at[slot, n], red.at[place, h, n], ps_sem.at[n, slot], pr_sem.at[n, place, h], owner
         )
         return owner, place, cp
+
+    def deliver(slot, n):
+        owner, place, cp = partial_copy(slot, n)
+
+        @pl.when(slot == own_slot)
+        def _():
+            red[place, h, n] = pbuf[slot, n]
+
+        far = first & (slot >= 1) & (slot <= 4)
+        pl.when((slot != own_slot) & jnp.logical_not(far))(lambda: cp.start())
+
+        @pl.when(far)
+        def _():
+            place = jnp.clip(slot - 1, 0, 3)
+            rcopy(
+                pbuf.at[slot, n], rbuf.at[place, n], ps_sem.at[n, slot], rr_sem.at[n, place],
+                z * 8 + 2 + h,
+            ).start()
 
     def second_pass(step, _):
         slot = step
@@ -374,15 +392,13 @@
         pl.when(slot != own_slot)(lambda: arrive(slot, 1))
         grad_tiles(dev, slot, store)
         dkv[0] = nt(gb[store], qrt[dev])
-        dkv[1] = nt(eb[store], dos[dev])
 
         @pl.when(jnp.logical_not(first) & (slot < 2 * x))
         def _():
             grad_tiles(0, slot, store - 1)
             dkv[0] += nt(gb[store - 1], qrt[0])
-            dkv[1] += nt(eb[store - 1], dos[0])
-
-        pbuf[slot] = dkv[...].astype(BF16)
+
+        pbuf[slot, 0] = dkv[0].astype(BF16)
         gains = jnp.zeros((1, D), F32)
         for j in range(4):
             place = pl.ds(4 * jnp.where(slot == 8, 0, slot) + j, 1)
@@ -398,25 +414,23 @@
                 0, keepdims=True,
             )
         kga[...] += gains
-        owner, place, cp = partial_copy(slot)
-
-        @pl.when(slot == own_slot)
-        def _():
-            red[place, h] = pbuf[slot]
-
-        far = first & (slot >= 1) & (slot <= 4)
-        pl.when((slot != own_slot) & jnp.logical_not(far))(lambda: cp.start())
-
-        @pl.when(far)
-        def _():
-            place = jnp.clip(slot - 1, 0, 3)
-            rcopy(
-                pbuf.at[slot], rbuf.at[place], ps_sem.at[slot], rr_sem.at[place], z * 8 + 2 + h
-            ).start()
-
+        deliver(slot, 0)
         return 0
 
     lax.fori_loop(0, slots, second_pass, 0)
+
+    def value_pass(slot, _):
+        dev = jnp.where(first & (slot < 8), 0, 1)
+        store = jnp.where(first, 8 - slot, 2 * (2 * x - slot))
+        dkv[1] = nt(eb[store], dos[dev])
+
+        @pl.when(jnp.logical_not(first) & (slot < 2 * x))
+        def _():
+            dkv[1] += nt(eb[store - 1], dos[0])
+
+        pbuf[slot, 1] = dkv[1].astype(BF16)
+        deliver(slot, 1)
+        return 0
 
     finish(1 - h)
     dq_far = rcopy(dqo.at[1 - h], dq_hbm.at[:, mine], os_sem, or_sem, partner)
@@ -454,30 +468,37 @@
         return jnp.sum(buf[...], 0)
 
     given = give(stages[0], total)
-    def passing(n):
+    def passing(m, n):
         return rcopy(
-            rbuf.at[n], red.at[0, h], fs_sem.at[n], pr_sem.at[0, h], zprev * 8 + 2 + n
+            rbuf.at[n, m], red.at[0, h, m], fs_sem.at[m, n], pr_sem.at[m, 0, h],
+            zprev * 8 + 2 + n,
         )
 
-    def relay(places):
+    def relay(m, places):
         @pl.when(x == 1)
         def _():
             for n in places:
-                rcopy(pbuf.at[0], rbuf.at[n], ps_sem.at[0], rr_sem.at[n], c).wait_recv()
-                passing(n).start()
-
-    relay((0, 1))
+                rcopy(
+                    pbuf.at[0, m], rbuf.at[n, m], ps_sem.at[m, 0], rr_sem.at[m, n], c
+                ).wait_recv()
+                passing(m, n).start()
+
+    lax.fori_loop(0, jnp.minimum(slots, 3), value_pass, 0)
+    relay(0, (0, 1, 2, 3))
     given += give(stages[1], collect(stages[0]))
-    relay((2,))
+    lax.fori_loop(3, jnp.minimum(slots, 6), value_pass, 0)
+    relay(1, (0, 1))
     given += give(stages[2], collect(stages[1]))
-    relay((3,))
+    lax.fori_loop(6, slots, value_pass, 0)
+    relay(1, (2, 3))
 
     own_place = jnp.where(first, 4, x)
 
     def take(place, head):
-        rcopy(
-            pbuf.at[0], red.at[place, head], ps_sem.at[0], pr_sem.at[place, head], c
-        ).wait_recv()
+        for n in range(2):
+            rcopy(
+                pbuf.at[0, n], red.at[place, head, n], ps_sem.at[n, 0], pr_sem.at[n, place, head], c
+            ).wait_recv()
 
     take(own_place, 1 - h)
     acc[...] = red[own_place].astype(F32)
@@ -512,15 +533,20 @@
         cp.wait_send()
 
     def drain(slot, _):
-        pl.when(slot != own_slot)(lambda: partial_copy(slot)[2].wait_send())
+        @pl.when(slot != own_slot)
+        def _():
+            for n in range(2):
+                partial_copy(slot, n)[2].wait_send()
+
         return 0
 
     lax.fori_loop(0, slots, drain, 0)
 
     @pl.when(x == 1)
     def _():
-        for n in range(4):
-            passing(n).wait_send()
+        for m in range(2):
+            for n in range(4):
+                passing(m, n).wait_send()
 
     dq_near.wait()
     dq_far.wait_send()
@@ -579,7 +605,7 @@
             V((2, 2, T, D), F32),
             V((8, 8, D), F32), V((4, 8, D), F32), V((nz, 8, D), F32),
             dma((3,)), dma((4,)), dma((4,)), dma((2, 9)), dma((2, 9)),
-            dma((9,)), dma((5, 2)), dma((4,)), dma((4,)), dma, dma,
+            dma((2, 9)), dma((2, 5, 2)), dma((2, 4)), dma((2, 4)), dma, dma,
             dma((7,)), dma((8,)), dma((3,)), dma((4,)), dma((nz - 1,)), dma((nz,)),
         ],
         compiler_params=pltpu.CompilerParams(

time: 58.8 us -> 57.5 us (0.978)
  Pallas kernels: 57.4 us -> 56.6 us
    pallas_call x1, Pallas kernels: 54 us -> 53.3 us  [on_device(): pl.pallas_call(functools.partial(kernel, nz), out_shape=(jax.ShapeDtypeSt...]
where the time goes in v5:
time: 57.5 us; the launch traced here: 57.2 us
  Pallas kernels  56.6 us (98%)
  between operations  0.64 us (1%)
    pallas_call x1, Pallas kernels, on_device(): pl.pallas_call(functools.partial(kernel, nz), out_shape=(jax.ShapeDtypeSt...  53.3 us
    pallas_call x1, Pallas kernels, on_device(): pl.pallas_call(emit, out_shape=(jax.ShapeDtypeStruct(q_raw.shape, BF16),...  3.33 us

profile of v5, /device:TPU:1, one launch (start us, length us, event | category | flops | bytes accessed | tf_op | source)
XLA Modules:
  0.0 57.2 jit_solution(9104868444275733697)
XLA Ops:
  0.6 53.3 %shard_map.128 = (bf16[256,2048]{1,0:T(8,128)(2,1)}, bf16[256,256]{1,0:T(8,128)(2,1)}, bf16[256,256]{1,0:T(8,128)(2,1)}, f32[1,128]{1,0:T(1,128)}, f32[1,128]{1,0:T(1,128)}) custom-call(bf16[256,2048]{1,0:T(8,128)(2,1)} %q_hbm.1, bf16[256,256]{1,0:T(8,128)(2,1)} %k_ref.1, bf16[256,256]{1,0:T(8,128)(2,1)} %v_ref.1, bf16[256,2048]{1,0:T(8,128)(2,1)} %so_hbm.1, ...), custom_call_target="tpu_custom_call" | custom-call | tf_op jit(solution)/shard_map/pallas_call | solution.py:583
  53.9 3.3 %shard_map.129 = (bf16[256,2048]{1,0:T(8,128)(2,1)}, bf16[256,256]{1,0:T(8,128)(2,1)}, bf16[256,256]{1,0:T(8,128)(2,1)}, f32[128]{0:T(128)}, f32[128]{0:T(128)}) custom-call(bf16[256,2048]{1,0:T(8,128)(2,1)} %get-tuple-element.10.dq, bf16[256,256]{1,0:T(8,128)(2,1)} %get-tuple-element.11.dk, bf16[256,256]{1,0:T(8,128)(2,1)} %get-tuple-element.12.dv, ...), custom_call_target="tpu_custom_call" | custom-call | tf_op jit(solution)/shard_map/pallas_call | solution.py:618
